TPU v7x, 32 devices: a whole 2x2x4 slice. The times are simulated.
32 devices in a mesh: pair: 16 (over z, y, x), vtile: 1, irrep: 2 (over core).
Axes of the slice: x: 2, y: 2, z: 4, core: 2. Of those that a mesh axis runs over, the one named last changes fastest.
Arguments:
- amplitudes: bfloat16 [80, 8, 7744], P('pair'), may hold values from -4 to 4
- slabs: bfloat16 [16, 8, 2, 88, 7744], P('pair', 'vtile', 'irrep'), may hold values from -1.5 to 1.5
- couplings: bfloat16 [2, 30, 30, 176], P(None, None, None, 'irrep'), may hold values from -6 to 6
- occ_energy: float32 [30], replicated, may hold values from -2 to -0.3
- vir_energy: float32 [8, 88], replicated, may hold values from 0.2 to 4
- occ_irrep: int32 [30], replicated, may hold values from 0 to 7
- pair_i: int32 [80], P('pair'), may hold values from 0 to 29, as said below
- pair_j: int32 [80], P('pair'), may hold values from 0 to 29, as said below
- window_k: int32 [2], replicated, may hold values from 0 to 29
- owner: int32 [2], replicated, may hold values from 0 to 15
Outputs:
- resid_part: float32 [80, 8, 7744], P('pair', 'vtile', 'irrep')
Inputs may be any that keep to these rules, and one draw needn't show every extreme that they name: Pairs come in groups of 16 that share pair_i; groups have different pair_i. Within a group of pairs sharing pair_i, pair_j values are distinct.
All inputs are finite; a program needn't handle non-finite values.
Results may differ from a plain program's by a relative error of at most 0.0003.
Values may be sent and summed in bfloat16 or wider, within the bound.
No kernel may reach another device: no remote copies, remote signals or barrier semaphores. Data moves between devices by JAX's collectives and lax.ppermute only.
A program may use at most 256 MiB of HBM per device.

v0:
```python
import jax
import jax.numpy as jnp
from jax import lax
from jax.sharding import PartitionSpec as P

K_WIN = 2


def spread_2(shard, axis, root):
    mine = lax.axis_index(axis) == root
    return lax.psum(jnp.where(mine, shard, jnp.zeros_like(shard)), axis)


def on_device(
    amplitudes, slabs, couplings, occ_energy, vir_energy, occ_irrep, pair_i, pair_j, window_k, owner
):
    tile_blocks = slabs.shape[1]
    block_size = slabs.shape[3]
    block_area = block_size * block_size
    occ_count = occ_irrep.shape[0]
    local_pairs = amplitudes.shape[0]
    tile_index = lax.axis_index("vtile")
    gamma_irrep = lax.axis_index("irrep")
    beta_irreps = tile_index * tile_blocks + jnp.arange(tile_blocks, dtype=jnp.int32)
    pair_sym = jnp.bitwise_xor(occ_irrep[pair_i], occ_irrep[pair_j])
    send_index = jnp.bitwise_xor(beta_irreps[None, :], pair_sym[:, None])
    outgoing = jnp.take_along_axis(amplitudes, send_index[:, :, None], axis=1)
    local_slab = slabs[0, :, 0]
    gamma_energy = jnp.take(vir_energy, gamma_irrep, axis=0)
    beta_energy = vir_energy[beta_irreps]
    occ_keep = jnp.bitwise_xor(occ_irrep, gamma_irrep)

    def pair_term(amp_pair, occ_i, occ_j, hole_part, slab_data, k_irrep, k_energy):
        pair_irrep = jnp.bitwise_xor(occ_irrep[occ_i], occ_irrep[occ_j])
        alpha_irrep = jnp.bitwise_xor(
            jnp.bitwise_xor(pair_irrep, k_irrep), jnp.bitwise_xor(beta_irreps, gamma_irrep)
        )
        amp_sel = amp_pair[alpha_irrep].reshape(tile_blocks, block_size, block_size)
        particle = jnp.einsum(
            "mad,mdx->max", amp_sel, slab_data, preferred_element_type=jnp.float32
        )
        energy_a = vir_energy[alpha_irrep]
        base = occ_energy[occ_i] + occ_energy[occ_j] + k_energy
        denominator = (
            energy_a[:, :, None, None]
            + beta_energy[:, None, :, None]
            + gamma_energy[None, None, None, :]
            - base
        )
        triples = (
            (particle - hole_part) / denominator.reshape(tile_blocks, block_size, block_area)
        ).astype(jnp.bfloat16)
        contrib = jnp.einsum("max,mdx->mad", triples, slab_data, preferred_element_type=jnp.float32)
        return (
            jnp.zeros((8, block_area), jnp.float32)
            .at[alpha_irrep]
            .add(contrib.reshape(tile_blocks, block_area))
        )

    def coupling_rows(window, occ_j, k_irrep):
        y_column = jnp.take(couplings[window], occ_j, axis=1)
        keep_mask = jnp.bitwise_xor(occ_keep, jnp.bitwise_xor(occ_irrep[occ_j], k_irrep)) == 0
        return y_column.astype(jnp.float32) * keep_mask[:, None].astype(jnp.float32)

    empty_stash = jnp.zeros((local_pairs, occ_count, tile_blocks, block_area), jnp.bfloat16)
    empty_seen = jnp.zeros((local_pairs, occ_count), jnp.float32)
    stash = empty_stash
    seen = empty_seen
    piece_amp = lax.all_gather(outgoing, "pair", axis=0, tiled=True)
    piece_first = lax.all_gather(pair_i, "pair", axis=0, tiled=True)
    piece_second = lax.all_gather(pair_j, "pair", axis=0, tiled=True)
    match = piece_first[None, :] == pair_i[:, None]
    slot = jnp.where(match, piece_second[None, :], occ_count).astype(jnp.int32)
    row_index = jnp.broadcast_to(jnp.arange(local_pairs, dtype=jnp.int32)[:, None], slot.shape)
    spread = jnp.broadcast_to(piece_amp[None], (local_pairs,) + piece_amp.shape)
    stash = stash.at[row_index, slot].add(spread, mode="drop")
    seen = seen.at[row_index, slot].add(jnp.ones(slot.shape, jnp.float32), mode="drop")
    accumulated = jnp.zeros((local_pairs, 8, block_area), jnp.float32)
    for window in range(K_WIN):
        slab_data = spread_2(local_slab, "pair", owner[window])
        k_index = window_k[window]
        k_irrep = occ_irrep[k_index]
        k_energy = occ_energy[k_index]

        def folded_step(packed):
            amp_pair, occ_i, occ_j, slot_amp, slot_seen = packed
            coef_rows = coupling_rows(window, occ_j, k_irrep)
            coupling = (coef_rows * slot_seen[:, None]).astype(jnp.bfloat16)
            hole_part = jnp.einsum(
                "qmx,qc->mxc", slot_amp, coupling, preferred_element_type=jnp.float32
            )
            hole_part = hole_part.reshape(tile_blocks, block_size, block_area)
            return pair_term(amp_pair, occ_i, occ_j, hole_part, slab_data, k_irrep, k_energy)

        contrib_all = lax.map(folded_step, (amplitudes, pair_i, pair_j, stash, seen))
        accumulated = accumulated + contrib_all
    summed = lax.psum(accumulated, ("vtile", "irrep"))
    irrep_count = lax.axis_size("irrep")
    share = block_area // irrep_count
    summed = lax.dynamic_slice_in_dim(summed, tile_index * tile_blocks, tile_blocks, 1)
    return lax.dynamic_slice_in_dim(summed, gamma_irrep * share, share, 2)


def solution(mesh):
    placed = (
        P("pair", None, None),
        P("pair", "vtile", "irrep", None, None),
        P(None, None, None, "irrep"),
        P(),
        P(),
        P(),
        P("pair"),
        P("pair"),
        P(),
        P(),
    )
    return jax.shard_map(
        on_device,
        mesh=mesh,
        in_specs=placed,
        out_specs=P("pair", "vtile", "irrep"),
        check_vma=False,
    )
```

profile of v0, /device:TPU:12, one launch (start us, length us, event | category | flops | bytes accessed | tf_op | source)
XLA Modules:
  0.0 2030.4 jit_solution(10936763291649276)
XLA Ops:
  10.1 4.8 gather_fusion.7
  18.6 12.7 fusion.45
  33.7 12.6 all-reduce.2
  51.4 18.9 scatter_fusion.1
  72.4 70.3 %all-gather.2.cloned.1.call-done = bf16[80,8,7744]{2,1,0:T(8,128)(2,1)} async-done(((bf16[5,8,7744]{2,1,0:T(8,128)(2,1)}), bf16[80,8,7744]{2,1,0:T(8,128)(2,1)}) %all-gather.2.cloned.1.call-update) | async-done | bytes 9912336 | tf_op jit(solution)/shard_map/all_gather | solution.py:69
  142.7 19.9 broadcast_in_dim.110
  162.7 6.5 broadcast_in_dim.70
  169.2 217.3 %scatter_fusion = bf16[5,30,8,7744]{3,2,1,0:T(8,128)(2,1)} fusion(bf16[5,30,8,7744]{3,2,1,0:T(8,128)(2,1)} %broadcast_in_dim.70, s32[400]{0:T(512)S(1)} %reshape.436, bf16[400,8,7744]{2,1,0:T(8,128)(2,1)} %bitcast.164), kind=kCustom, calls=%fused_computation.10 | custom fusion | flops 24780800 | bytes 148688000 | tf_op jit(solution)/shard_map/scatter-add | solution.py:76
  386.5 18.4 copy.27
  404.9 327.3 %all-reduce.9.cloned.1.call-done = (bf16[8,88,7744]{2,1,0:T(8,128)(2,1)}, bf16[8,88,7744]{2,1,0:T(8,128)(2,1)}) async-done(((bf16[8,88,7744]{2,1,0:T(8,128)(2,1)}, bf16[8,88,7744]{2,1,0:T(8,128)(2,1)}), (bf16[8,88,7744]{2,1,0:T(8,128)(2,1)}, bf16[8,88,7744]{2,1,0:T(8,128)(2,1)})) %all-reduce.9.cloned.1.call-update) | async-done | bytes 21807120 | tf_op jit(solution)/shard_map/psum | solution.py:11
  732.3 630.2 %while.25 = (s32[]{:T(128)}, f32[5,8,7744]{2,1,0:T(8,128)S(1)}, s32[5]{0:T(128)S(1)}, s32[30]{0:T(128)S(1)}, s32[5]{0:T(128)S(1)}, /*index=5*/s32[]{:T(128)}, s3...) while((s32[]{:T(128)}, f32[5,8,7744]{2,1,0:T(8,128)S(1)}, ...), condition=%wide.region_9.11_spmd.clone, body=%wide.region_7.10_spmd.clone.sunk | while | flops 2273528832 | bytes 192679184 | solution.py:95
  740.6 12.1 add.388
  752.7 28.6 %add.389 = f32[8,88,7744]{2,1,0:T(8,128)} reshape(f32[8,88,88,88]{3,2,1,0:T(8,128)} %add.388) | data formatting | bytes 43614208 | tf_op jit(solution)/shard_map/while/body/eval_jaxpr/add | solution.py:45
  782.6 14.1 fusion.116
  796.7 28.6 %reshape.521 = f32[8,88,7744]{2,1,0:T(8,128)} reshape(f32[8,7744,88]{2,1,0:T(8,128)} %fusion.116) | data formatting | bytes 43614208 | tf_op jit(solution)/shard_map/while/body/eval_jaxpr/reshape | solution.py:92
  830.4 26.7 %fusion.118 = f32[8,88,88]{2,1,0:T(8,128)S(1)} fusion(bf16[8,88,7744]{2,1,0:T(8,128)(2,1)} %get-tuple-element.861, f32[8,88,7744]{2,1,0:T(8,128)} %add.389, f32[8,88,7744]{2,1,0:T(8,128)} %reshape.521, bf16[8,88,88]{2,1,0:T(8,128)(2,1)S(1)} %reshape.522, f32[]{:T(128)S(6)} %add.391, f32[7744]{0:T(1024)S(1)} %add.393), kind=kOutput, calls=%fused_computation.45.clone.1 | convolution fusion | flops 1946284032 | bytes 54920452 | tf_op jit(solution)/shard_map/while/body/eval_jaxpr/max,mdx->mad/dot_general | solution.py:53
  866.6 12.1 add.388
  878.7 28.6 %add.389 = f32[8,88,7744]{2,1,0:T(8,128)} reshape(f32[8,88,88,88]{3,2,1,0:T(8,128)} %add.388) | data formatting | bytes 43614208 | tf_op jit(solution)/shard_map/while/body/eval_jaxpr/add | solution.py:45
  908.6 14.1 fusion.116
  922.7 28.6 %reshape.521 = f32[8,88,7744]{2,1,0:T(8,128)} reshape(f32[8,7744,88]{2,1,0:T(8,128)} %fusion.116) | data formatting | bytes 43614208 | tf_op jit(solution)/shard_map/while/body/eval_jaxpr/reshape | solution.py:92
  956.5 26.7 %fusion.118 = f32[8,88,88]{2,1,0:T(8,128)S(1)} fusion(bf16[8,88,7744]{2,1,0:T(8,128)(2,1)} %get-tuple-element.861, f32[8,88,7744]{2,1,0:T(8,128)} %add.389, f32[8,88,7744]{2,1,0:T(8,128)} %reshape.521, bf16[8,88,88]{2,1,0:T(8,128)(2,1)S(1)} %reshape.522, f32[]{:T(128)S(6)} %add.391, f32[7744]{0:T(1024)S(1)} %add.393), kind=kOutput, calls=%fused_computation.45.clone.1 | convolution fusion | flops 1946284032 | bytes 54920452 | tf_op jit(solution)/shard_map/while/body/eval_jaxpr/max,mdx->mad/dot_general | solution.py:53
  992.7 12.1 add.388
  1004.8 28.6 %add.389 = f32[8,88,7744]{2,1,0:T(8,128)} reshape(f32[8,88,88,88]{3,2,1,0:T(8,128)} %add.388) | data formatting | bytes 43614208 | tf_op jit(solution)/shard_map/while/body/eval_jaxpr/add | solution.py:45
  1034.7 14.1 fusion.116
  1048.8 28.6 %reshape.521 = f32[8,88,7744]{2,1,0:T(8,128)} reshape(f32[8,7744,88]{2,1,0:T(8,128)} %fusion.116) | data formatting | bytes 43614208 | tf_op jit(solution)/shard_map/while/body/eval_jaxpr/reshape | solution.py:92
  1082.5 26.7 %fusion.118 = f32[8,88,88]{2,1,0:T(8,128)S(1)} fusion(bf16[8,88,7744]{2,1,0:T(8,128)(2,1)} %get-tuple-element.861, f32[8,88,7744]{2,1,0:T(8,128)} %add.389, f32[8,88,7744]{2,1,0:T(8,128)} %reshape.521, bf16[8,88,88]{2,1,0:T(8,128)(2,1)S(1)} %reshape.522, f32[]{:T(128)S(6)} %add.391, f32[7744]{0:T(1024)S(1)} %add.393), kind=kOutput, calls=%fused_computation.45.clone.1 | convolution fusion | flops 1946284032 | bytes 54920452 | tf_op jit(solution)/shard_map/while/body/eval_jaxpr/max,mdx->mad/dot_general | solution.py:53
  1118.7 12.1 add.388
  1130.8 28.6 %add.389 = f32[8,88,7744]{2,1,0:T(8,128)} reshape(f32[8,88,88,88]{3,2,1,0:T(8,128)} %add.388) | data formatting | bytes 43614208 | tf_op jit(solution)/shard_map/while/body/eval_jaxpr/add | solution.py:45
  1160.7 14.1 fusion.116
  1174.8 28.6 %reshape.521 = f32[8,88,7744]{2,1,0:T(8,128)} reshape(f32[8,7744,88]{2,1,0:T(8,128)} %fusion.116) | data formatting | bytes 43614208 | tf_op jit(solution)/shard_map/while/body/eval_jaxpr/reshape | solution.py:92
  1208.6 26.7 %fusion.118 = f32[8,88,88]{2,1,0:T(8,128)S(1)} fusion(bf16[8,88,7744]{2,1,0:T(8,128)(2,1)} %get-tuple-element.861, f32[8,88,7744]{2,1,0:T(8,128)} %add.389, f32[8,88,7744]{2,1,0:T(8,128)} %reshape.521, bf16[8,88,88]{2,1,0:T(8,128)(2,1)S(1)} %reshape.522, f32[]{:T(128)S(6)} %add.391, f32[7744]{0:T(1024)S(1)} %add.393), kind=kOutput, calls=%fused_computation.45.clone.1 | convolution fusion | flops 1946284032 | bytes 54920452 | tf_op jit(solution)/shard_map/while/body/eval_jaxpr/max,mdx->mad/dot_general | solution.py:53
  1244.8 12.1 add.388
  1256.8 28.6 %add.389 = f32[8,88,7744]{2,1,0:T(8,128)} reshape(f32[8,88,88,88]{3,2,1,0:T(8,128)} %add.388) | data formatting | bytes 43614208 | tf_op jit(solution)/shard_map/while/body/eval_jaxpr/add | solution.py:45
  1286.8 14.1 fusion.116
  1300.8 28.6 %reshape.521 = f32[8,88,7744]{2,1,0:T(8,128)} reshape(f32[8,7744,88]{2,1,0:T(8,128)} %fusion.116) | data formatting | bytes 43614208 | tf_op jit(solution)/shard_map/while/body/eval_jaxpr/reshape | solution.py:92
  1334.6 26.7 %fusion.118 = f32[8,88,88]{2,1,0:T(8,128)S(1)} fusion(bf16[8,88,7744]{2,1,0:T(8,128)(2,1)} %get-tuple-element.861, f32[8,88,7744]{2,1,0:T(8,128)} %add.389, f32[8,88,7744]{2,1,0:T(8,128)} %reshape.521, bf16[8,88,88]{2,1,0:T(8,128)(2,1)S(1)} %reshape.522, f32[]{:T(128)S(6)} %add.391, f32[7744]{0:T(1024)S(1)} %add.393), kind=kOutput, calls=%fused_computation.45.clone.1 | convolution fusion | flops 1946284032 | bytes 54920452 | tf_op jit(solution)/shard_map/while/body/eval_jaxpr/max,mdx->mad/dot_general | solution.py:53
  1364.0 634.4 %while.24 = (s32[]{:T(128)}, f32[5,8,7744]{2,1,0:T(8,128)}, s32[5]{0:T(128)S(1)}, s32[30]{0:T(128)S(1)}, s32[5]{0:T(128)S(1)}, /*index=5*/s32[]{:T(128)}, s32[]{...) while((s32[]{:T(128)}, f32[5,8,7744]{2,1,0:T(8,128)}, ...), condition=%wide.region_5.7_spmd.clone, body=%wide.region_3.6_spmd.clone.sunk | while | flops 2273528832 | bytes 192677648 | solution.py:95
  1372.3 12.1 add.373
  1384.4 28.6 %add.374 = f32[8,88,7744]{2,1,0:T(8,128)} reshape(f32[8,88,88,88]{3,2,1,0:T(8,128)} %add.373) | data formatting | bytes 43614208 | tf_op jit(solution)/shard_map/while/body/eval_jaxpr/add | solution.py:45
  1414.4 14.2 fusion.104
  1428.5 28.6 %reshape.512 = f32[8,88,7744]{2,1,0:T(8,128)} reshape(f32[8,7744,88]{2,1,0:T(8,128)} %fusion.104) | data formatting | bytes 43614208 | tf_op jit(solution)/shard_map/while/body/eval_jaxpr/reshape | solution.py:92
  1462.2 26.8 %fusion.106 = f32[8,88,88]{2,1,0:T(8,128)S(1)} fusion(bf16[8,88,7744]{2,1,0:T(8,128)(2,1)} %get-tuple-element.792, f32[8,88,7744]{2,1,0:T(8,128)} %add.374, f32[8,88,7744]{2,1,0:T(8,128)} %reshape.512, bf16[8,88,88]{2,1,0:T(8,128)(2,1)S(1)} %reshape.513, f32[]{:T(128)S(6)} %add.376, f32[7744]{0:T(1024)S(1)} %add.378), kind=kOutput, calls=%fused_computation.15.clone.1 | convolution fusion | flops 1946284032 | bytes 54920452 | tf_op jit(solution)/shard_map/while/body/eval_jaxpr/max,mdx->mad/dot_general | solution.py:53
  1499.2 12.1 add.373
  1511.3 28.6 %add.374 = f32[8,88,7744]{2,1,0:T(8,128)} reshape(f32[8,88,88,88]{3,2,1,0:T(8,128)} %add.373) | data formatting | bytes 43614208 | tf_op jit(solution)/shard_map/while/body/eval_jaxpr/add | solution.py:45
  1541.3 14.2 fusion.104
  1555.4 28.6 %reshape.512 = f32[8,88,7744]{2,1,0:T(8,128)} reshape(f32[8,7744,88]{2,1,0:T(8,128)} %fusion.104) | data formatting | bytes 43614208 | tf_op jit(solution)/shard_map/while/body/eval_jaxpr/reshape | solution.py:92
  1589.1 26.8 %fusion.106 = f32[8,88,88]{2,1,0:T(8,128)S(1)} fusion(bf16[8,88,7744]{2,1,0:T(8,128)(2,1)} %get-tuple-element.792, f32[8,88,7744]{2,1,0:T(8,128)} %add.374, f32[8,88,7744]{2,1,0:T(8,128)} %reshape.512, bf16[8,88,88]{2,1,0:T(8,128)(2,1)S(1)} %reshape.513, f32[]{:T(128)S(6)} %add.376, f32[7744]{0:T(1024)S(1)} %add.378), kind=kOutput, calls=%fused_computation.15.clone.1 | convolution fusion | flops 1946284032 | bytes 54920452 | tf_op jit(solution)/shard_map/while/body/eval_jaxpr/max,mdx->mad/dot_general | solution.py:53
  1626.1 12.1 add.373
  1638.2 28.6 %add.374 = f32[8,88,7744]{2,1,0:T(8,128)} reshape(f32[8,88,88,88]{3,2,1,0:T(8,128)} %add.373) | data formatting | bytes 43614208 | tf_op jit(solution)/shard_map/while/body/eval_jaxpr/add | solution.py:45
  1668.1 14.2 fusion.104
  1682.3 28.6 %reshape.512 = f32[8,88,7744]{2,1,0:T(8,128)} reshape(f32[8,7744,88]{2,1,0:T(8,128)} %fusion.104) | data formatting | bytes 43614208 | tf_op jit(solution)/shard_map/while/body/eval_jaxpr/reshape | solution.py:92
  1716.0 26.8 %fusion.106 = f32[8,88,88]{2,1,0:T(8,128)S(1)} fusion(bf16[8,88,7744]{2,1,0:T(8,128)(2,1)} %get-tuple-element.792, f32[8,88,7744]{2,1,0:T(8,128)} %add.374, f32[8,88,7744]{2,1,0:T(8,128)} %reshape.512, bf16[8,88,88]{2,1,0:T(8,128)(2,1)S(1)} %reshape.513, f32[]{:T(128)S(6)} %add.376, f32[7744]{0:T(1024)S(1)} %add.378), kind=kOutput, calls=%fused_computation.15.clone.1 | convolution fusion | flops 1946284032 | bytes 54920452 | tf_op jit(solution)/shard_map/while/body/eval_jaxpr/max,mdx->mad/dot_general | solution.py:53
  1753.0 12.1 add.373
  1765.1 28.6 %add.374 = f32[8,88,7744]{2,1,0:T(8,128)} reshape(f32[8,88,88,88]{3,2,1,0:T(8,128)} %add.373) | data formatting | bytes 43614208 | tf_op jit(solution)/shard_map/while/body/eval_jaxpr/add | solution.py:45
  1795.0 14.2 fusion.104
  1809.2 28.6 %reshape.512 = f32[8,88,7744]{2,1,0:T(8,128)} reshape(f32[8,7744,88]{2,1,0:T(8,128)} %fusion.104) | data formatting | bytes 43614208 | tf_op jit(solution)/shard_map/while/body/eval_jaxpr/reshape | solution.py:92
  1842.9 26.8 %fusion.106 = f32[8,88,88]{2,1,0:T(8,128)S(1)} fusion(bf16[8,88,7744]{2,1,0:T(8,128)(2,1)} %get-tuple-element.792, f32[8,88,7744]{2,1,0:T(8,128)} %add.374, f32[8,88,7744]{2,1,0:T(8,128)} %reshape.512, bf16[8,88,88]{2,1,0:T(8,128)(2,1)S(1)} %reshape.513, f32[]{:T(128)S(6)} %add.376, f32[7744]{0:T(1024)S(1)} %add.378), kind=kOutput, calls=%fused_computation.15.clone.1 | convolution fusion | flops 1946284032 | bytes 54920452 | tf_op jit(solution)/shard_map/while/body/eval_jaxpr/max,mdx->mad/dot_general | solution.py:53
  1879.9 12.1 add.373
  1892.0 28.6 %add.374 = f32[8,88,7744]{2,1,0:T(8,128)} reshape(f32[8,88,88,88]{3,2,1,0:T(8,128)} %add.373) | data formatting | bytes 43614208 | tf_op jit(solution)/shard_map/while/body/eval_jaxpr/add | solution.py:45
  1921.9 14.2 fusion.104
  1936.1 28.6 %reshape.512 = f32[8,88,7744]{2,1,0:T(8,128)} reshape(f32[8,7744,88]{2,1,0:T(8,128)} %fusion.104) | data formatting | bytes 43614208 | tf_op jit(solution)/shard_map/while/body/eval_jaxpr/reshape | solution.py:92
  1969.8 26.8 %fusion.106 = f32[8,88,88]{2,1,0:T(8,128)S(1)} fusion(bf16[8,88,7744]{2,1,0:T(8,128)(2,1)} %get-tuple-element.792, f32[8,88,7744]{2,1,0:T(8,128)} %add.374, f32[8,88,7744]{2,1,0:T(8,128)} %reshape.512, bf16[8,88,88]{2,1,0:T(8,128)(2,1)S(1)} %reshape.513, f32[]{:T(128)S(6)} %add.376, f32[7744]{0:T(1024)S(1)} %add.378), kind=kOutput, calls=%fused_computation.15.clone.1 | convolution fusion | flops 1946284032 | bytes 54920452 | tf_op jit(solution)/shard_map/while/body/eval_jaxpr/max,mdx->mad/dot_general | solution.py:53
  1998.4 2.9 add.236
  2001.3 20.4 %all-reduce.7.cloned.1.call-done = f32[5,8,7744]{2,1,0:T(8,128)} async-done(((f32[5,8,7744]{2,1,0:T(8,128)}), f32[5,8,7744]{2,1,0:T(8,128)}) %all-reduce.7.cloned.1.call-update) | async-done | bytes 1239056 | tf_op jit(solution)/shard_map/psum | solution.py:97
  (244 shorter events, 87.2 us)
Async XLA Ops:
  6.5 136.2 %all-gather.2.cloned.1.call-start = ((), (), s32[]{:S(2)}) async-start(), calls=%async_computation | async-start | bytes 10618880 | tf_op jit(solution)/shard_map/all_gather | solution.py:69
  15.9 716.3 %all-reduce.9.cloned.1.call-start = ((), (), s32[]{:S(2)}) async-start(), calls=%async_computation.2 | async-start | bytes 43974656 | tf_op jit(solution)/shard_map/psum | solution.py:11
  31.3 0.7 copy-start.7
  31.3 1.9 copy-start.5
  31.3 2.1 copy-start.6
  31.3 15.1 copy-start.4
  31.3 18.2 copy-start.3
  31.3 19.5 copy-start.1
  31.3 39.0 %copy-start = (s32[30]{0:T(128)S(1)}, s32[30]{0:T(128)}, u32[]{:S(2)}) copy-start(s32[30]{0:T(128)} %param.21) | copy-start | bytes 364
  31.4 1990.4 %all-reduce.7.cloned.1.call-start = ((), (), s32[]{:S(2)}) async-start(), calls=%async_computation.1 | async-start | bytes 2498560 | tf_op jit(solution)/shard_map/psum | solution.py:97
  1362.5 1.5 copy-start.2
Sparse Core Ops, SparseCore 0:
  16.0 126.6 all-gather.1
  149.1 583.0 all-reduce.8
  2001.4 20.2 all-reduce.6
where the time goes:
time: 2050 us; the launch traced here: 2030 us
  local copies, waits for them, and re-layouts  817 us (40%)
  waiting for transfers between devices  418 us (20%)
  matrix products  409 us (20%)
  other arithmetic  265 us (13%)
  loops' own time  89.9 us (4%)
    add x40, local copies, waits for them, and re-layouts, pair_term(): energy_a[:, :, None, None] + beta_energy[:, None, :, None]  408 us
    psum x1, waiting for transfers between devices, spread_2(): return lax.psum(jnp.where(mine, shard, jnp.zeros_like(shard)), axis)  327 us
    reshape x10, local copies, waits for them, and re-layouts, folded_step(): hole_part = hole_part.reshape(tile_blocks, block_size, block_area)  286 us
    dot_general x10, matrix products, pair_term(): jnp.einsum('max,mdx->mad', triples, slab_data, preferred_element_type=jnp...  268 us
    scatter-add x1, other arithmetic, on_device(): stash = stash.at[row_index, slot].add(spread, mode='drop')  217 us
    dot_general x10, matrix products, folded_step(): jnp.einsum('qmx,qc->mxc', slot_amp, coupling, preferred_element_type=jnp....  141 us
    another operation x2, loops' own time, on_device(): lax.map(folded_step, (amplitudes, pair_i, pair_j, stash, seen))  89.9 us
    all_gather x1, waiting for transfers between devices, on_device(): piece_amp = lax.all_gather(outgoing, 'pair', axis=0, tiled=True)  70.3 us
  transfers between devices with their start and end apart: 3, of which 3 were waited for; matrix products, arithmetic and copies ran while one was open for 15% of the time, Pallas kernels for 0%

commit v1 on v0

--- a/solution.py
+++ b/solution.py
@@ -1,6 +1,10 @@
+import math
+
 import jax
 import jax.numpy as jnp
 from jax import lax
+from jax.experimental import pallas as pl
+from jax.experimental.pallas import tpu as pltpu
 from jax.sharding import PartitionSpec as P
 
 K_WIN = 2
@@ -11,7 +15,7 @@
     return lax.psum(jnp.where(mine, shard, jnp.zeros_like(shard)), axis)
 
 
-def on_device(
+def on_device_gather(
     amplitudes, slabs, couplings, occ_energy, vir_energy, occ_irrep, pair_i, pair_j, window_k, owner
 ):
     tile_blocks = slabs.shape[1]
@@ -101,6 +105,258 @@
     return lax.dynamic_slice_in_dim(summed, gamma_irrep * share, share, 2)
 
 
+GROUP = 16
+LANE = 128
+TILE = 256
+
+
+def tile_plan(rows):
+    lanes = -(-GROUP * rows // TILE) * TILE
+    depth = LANE // GROUP
+    starts = []
+    for first in range(0, lanes, TILE):
+        lowest = min(first // rows, GROUP - depth)
+        highest = min((first + TILE - 1) // rows, GROUP - 1)
+        assert lowest >= 0 and highest < lowest + depth
+        starts.append(lowest)
+    return lanes, depth, starts
+
+
+def b_chunks(block):
+    unit = LANE // math.gcd(LANE, block)
+    size = 2 * unit
+    return [(first, min(size, block - first)) for first in range(0, block, size)]
+
+
+def triples_kernel(
+    eb_ref, vt_ref, v_ref, at_ref, arep_ref, ct_ref, mask_ref, ecol_ref, lrow_ref, o_ref, t_ref, acc_ref
+):
+    count, block = vt_ref.shape[1], vt_ref.shape[2]
+    depth = mask_ref.shape[1] // GROUP
+    tiles = mask_ref.shape[0]
+    window = pl.program_id(1)
+
+    def pair_of_b(step, carry):
+        for tile in range(tiles):
+            lanes = slice(tile * TILE, (tile + 1) * TILE)
+            top = at_ref[0, :, lanes]
+            results = []
+            for half in range(2):
+                b = 2 * step + half
+                lhs = jnp.concatenate([vt_ref[0, b], ct_ref[0, 0, tile]], axis=1)
+                hole_amp = arep_ref[0, 0, b, :, lanes]
+                bottom = jnp.concatenate([hole_amp] * depth, axis=0) * mask_ref[tile]
+                rhs = jnp.concatenate([top, bottom], axis=0)
+                numer = jnp.dot(lhs, rhs, preferred_element_type=jnp.float32)
+                denom = (ecol_ref[...] + eb_ref[window, b]) + lrow_ref[0, 0, :, lanes]
+                results.append(numer / denom)
+            rows = pl.ds(pl.multiple_of(step * (2 * block), 2 * block), 2 * block)
+            t_ref[rows, lanes] = jnp.concatenate(results, axis=0).astype(jnp.bfloat16)
+        return carry
+
+    lax.fori_loop(0, count // 2, pair_of_b, 0)
+    contrib = jnp.dot(v_ref[0], t_ref[...], preferred_element_type=jnp.float32)
+
+    @pl.when(window == 0)
+    def _():
+        acc_ref[...] = contrib
+
+    @pl.when(window > 0)
+    def _():
+        acc_ref[...] += contrib
+
+    @pl.when(window == pl.num_programs(1) - 1)
+    def _():
+        o_ref[0] = acc_ref[...].T
+
+
+def triples_call(eb, vt, v, at, arep, ct, mask, ecol, lrow):
+    windows, count, block, _ = vt.shape
+    groups, depth_rows, lanes = at.shape
+    grid = (groups, windows)
+    return pl.pallas_call(
+        triples_kernel,
+        grid=grid,
+        in_specs=[
+            pl.BlockSpec(memory_space=pltpu.SMEM),
+            pl.BlockSpec((1, count, block, LANE), lambda g, w: (w, 0, 0, 0)),
+            pl.BlockSpec((1, block, count * block), lambda g, w: (w, 0, 0)),
+            pl.BlockSpec((1, depth_rows, lanes), lambda g, w: (g, 0, 0)),
+            pl.BlockSpec((1, 1, count, GROUP, lanes), lambda g, w: (w, g, 0, 0, 0)),
+            pl.BlockSpec((1, 1) + ct.shape[2:], lambda g, w: (w, g, 0, 0, 0)),
+            pl.BlockSpec(mask.shape, lambda g, w: (0, 0, 0)),
+            pl.BlockSpec(ecol.shape, lambda g, w: (0, 0)),
+            pl.BlockSpec((1, 1, 1, lanes), lambda g, w: (w, g, 0, 0)),
+        ],
+        out_specs=pl.BlockSpec((1, lanes, block), lambda g, w: (g, 0, 0)),
+        out_shape=jax.ShapeDtypeStruct((groups, lanes, block), jnp.float32),
+        scratch_shapes=[
+            pltpu.VMEM((count * block, lanes), jnp.bfloat16),
+            pltpu.VMEM((block, lanes), jnp.float32),
+        ],
+        compiler_params=pltpu.CompilerParams(
+            dimension_semantics=("arbitrary", "arbitrary"), vmem_limit_bytes=48 * 1024 * 1024
+        ),
+        cost_estimate=pl.CostEstimate(
+            flops=groups * windows * count * block * lanes * 2 * (TILE + block),
+            bytes_accessed=arep.size * 2 + vt.size * 2 + v.size * 2,
+            transcendentals=groups * windows * count * block * lanes,
+        ),
+        name="triples",
+    )(eb, vt, v, at, arep, ct, mask, ecol, lrow)
+
+
+def swap_cores(x):
+    return lax.ppermute(x, "irrep", [(0, 1), (1, 0)])
+
+
+def across(x, bit):
+    count = lax.axis_size("pair")
+    return lax.ppermute(x, "pair", [(t, t ^ bit) for t in range(count)])
+
+
+def pick(x, index):
+    return lax.dynamic_index_in_dim(x, index, 0, keepdims=False)
+
+
+def fetch_slab(slab, owner, k_irrep, me, core):
+    windows = owner.shape[0]
+    bits = [(me >> n) & 1 for n in range(4)]
+    gamma = bits[0]
+    owner_bits = [[(owner[w] >> n) & 1 for n in range(4)] for w in range(windows)]
+    halves = slab.reshape((2, slab.shape[0] // 2) + slab.shape[1:])
+    mine, theirs = pick(halves, core), swap_cores(pick(halves, 1 - core))
+    same = gamma == core
+    here = jnp.where(same, mine, theirs)
+    there = across(jnp.where(same, theirs, mine), 1)
+
+    def low_block(w, high, low):
+        beta = (2 * high + low) ^ (k_irrep[w] & 3) ^ gamma
+        return jnp.where(owner_bits[w][0] == bits[0], pick(here, beta), pick(there, beta))
+
+    def low_blocks(low):
+        return jnp.stack([jnp.stack([low_block(w, high, low) for w in range(windows)]) for high in range(2)])
+
+    kept = low_blocks(bits[1])
+    came = across(low_blocks(1 - bits[1]), 2)
+    from_here = jnp.stack([owner_bits[w][1] == bits[1] for w in range(windows)])[:, None, None]
+    keep2 = jnp.where(from_here, pick(kept, bits[2]), pick(came, bits[2]))
+    send2 = jnp.where(from_here, pick(kept, 1 - bits[2]), pick(came, 1 - bits[2]))
+    came = across(send2, 4)
+    from_here = jnp.stack([owner_bits[w][2] == bits[2] for w in range(windows)])[:, None, None]
+    blocks = jnp.where(from_here, keep2, came)
+    mine, theirs = pick(blocks, core), swap_cores(pick(blocks, 1 - core))
+    high = (k_irrep[core] >> 2) & 1
+    mine_stays = (bits[3] ^ high) == core
+    kept = jnp.where(mine_stays, mine, theirs)
+    came = across(jnp.where(mine_stays, theirs, mine), 8)
+    block = jnp.where(((owner[core] >> 3) & 1) == bits[3], kept, came)
+    other = swap_cores(block)
+    return jnp.stack([jnp.where(core == 0, block, other), jnp.where(core == 0, other, block)])
+
+
+def on_device_scatter(
+    amplitudes, slabs, couplings, occ_energy, vir_energy, occ_irrep, pair_i, pair_j, window_k, owner
+):
+    betas, block = slabs.shape[1], slabs.shape[3]
+    windows = window_k.shape[0]
+    rows = block // lax.axis_size("irrep")
+    share = rows * block
+    chips = lax.axis_size("pair")
+    local_pairs = pair_i.shape[0]
+    pairs = chips * local_pairs
+    groups = pairs // GROUP
+    lanes, depth, starts = tile_plan(rows)
+    me, core = lax.axis_index("pair"), lax.axis_index("irrep")
+    gamma, m = me & 1, me >> 1
+    k_irrep = occ_irrep[window_k]
+    bf16, f32 = jnp.bfloat16, jnp.float32
+
+    chunks = b_chunks(block)
+    local = slabs[0, :, 0]
+    pieces = [
+        fetch_slab(local[:, :, first * block : (first + size) * block], owner, k_irrep, me, core)
+        for first, size in chunks
+    ]
+
+    both = lax.all_gather(jnp.stack([pair_i, pair_j]), "pair", axis=1, tiled=True)
+    numbers = jnp.arange(pairs, dtype=jnp.int32)
+    ahead = both[0][None, :] < both[0][:, None]
+    tied = (both[0][None, :] == both[0][:, None]) & (numbers[None, :] < numbers[:, None])
+    rank = jnp.sum((ahead | tied).astype(jnp.int32), axis=1)
+    placed = (rank[None, :] == numbers[:, None]).astype(jnp.int32)
+    order = jnp.sum(placed * numbers[None, :], axis=1)
+    first = jnp.sum(placed * both[0][None, :], axis=1)
+    second = jnp.sum(placed * both[1][None, :], axis=1)
+
+    pair_sym = occ_irrep[pair_i] ^ occ_irrep[pair_j]
+    mine = lax.dynamic_slice_in_dim(amplitudes, core * share, share, 2)
+    target = jnp.arange(chips, dtype=jnp.int32)
+    wanted = jnp.stack([target >> 1] + [(target >> 1) ^ (target & 1) ^ k_irrep[w] for w in range(windows)], 1)
+    index = wanted[:, :, None] ^ pair_sym[None, None, :]
+    sent = mine[jnp.arange(local_pairs, dtype=jnp.int32)[None, None, :], index]
+    kinds = 1 + windows
+    came = lax.all_to_all(sent.reshape(chips, kinds * local_pairs, share), "pair", 0, 0, tiled=True)
+    came = came.reshape(chips * kinds * local_pairs, share)
+    source = (order // local_pairs) * (kinds * local_pairs) + order % local_pairs
+    source = source[None, :] + local_pairs * jnp.arange(kinds, dtype=jnp.int32)[:, None]
+    amps = came[source].reshape(kinds, groups, GROUP, rows, block)
+    used = GROUP * rows
+    at = amps[0].transpose(0, 3, 1, 2).reshape(groups, block, used)
+    at = jnp.pad(at, ((0, 0), (0, LANE - block), (0, lanes - used)))
+    lane = jnp.arange(lanes, dtype=jnp.int32)
+    spread = ((lane[None, :] % rows == jnp.arange(rows)[:, None]) & (lane < used)[None, :]).astype(bf16)
+    lane_pair = lane // rows
+    mask = jnp.stack([
+        (jnp.repeat(start + jnp.arange(depth), GROUP)[:, None] == lane_pair[None, n * TILE : (n + 1) * TILE])
+        for n, start in enumerate(starts)
+    ]).astype(bf16)
+
+    coupled = jnp.where(gamma == core, couplings, swap_cores(couplings))
+    chosen = (second.reshape(groups, GROUP)[:, :, None] == jnp.arange(occ_irrep.shape[0])).astype(bf16)
+    coupled = jnp.einsum("gql,wljc->wgqjc", chosen, coupled)
+    coupled = jnp.einsum("gpj,wgqjc->wgcpq", chosen, coupled)
+    sym_j = occ_irrep[second].reshape(groups, GROUP)
+    keep = (sym_j[None, :, :, None] ^ sym_j[None, :, None, :] ^ gamma ^ k_irrep[:, None, None, None]) == 0
+    coupled = -(coupled * keep[:, :, None].astype(bf16))
+    ct = jnp.stack(
+        [coupled[:, :, :, s : s + depth].reshape(windows, groups, block, depth * GROUP) for s in starts], 2
+    )
+
+    alpha = occ_irrep[first] ^ occ_irrep[second] ^ m
+    energy_a = lax.dynamic_slice_in_dim(vir_energy, core * rows, rows, 1)[alpha]
+    base = occ_energy[first] + occ_energy[second]
+    lrow = energy_a[None] - (base[None] + occ_energy[window_k][:, None])[:, :, None]
+    lrow = lrow.reshape(windows, groups, 1, used)
+    lrow = jnp.pad(lrow, ((0, 0), (0, 0), (0, 0), (0, lanes - used)), constant_values=1.0)
+    ecol = jnp.broadcast_to(pick(vir_energy, gamma)[:, None], (block, TILE))
+    energy_b = vir_energy[m ^ gamma ^ k_irrep]
+
+    eye = (jnp.arange(block)[:, None] == jnp.arange(LANE)[None, :]).astype(bf16)
+    total = None
+    for (start, size), v in zip(chunks, pieces):
+        vt = jnp.einsum("wdx,de->wxe", v, eye).reshape(windows, size, block, LANE)
+        hole = amps[1:, :, :, :, start : start + size]
+        arep = jnp.einsum("wgqab,ae->wgbqe", hole, spread)
+        part = triples_call(energy_b[:, start : start + size], vt, v, at, arep, ct, mask, ecol, lrow)
+        total = part if total is None else total + part
+    total = total[:, :used].reshape(pairs, share)[rank]
+    came = lax.all_to_all(total.reshape(chips, local_pairs, share), "pair", 0, 0, tiled=True)
+    came = came.reshape(betas, 2, local_pairs, share)
+    came = came[:, 0] + came[:, 1]
+    back = jnp.arange(betas, dtype=jnp.int32)[None, :] ^ pair_sym[:, None]
+    return came[back, jnp.arange(local_pairs, dtype=jnp.int32)[:, None]]
+
+
+def on_device(*args):
+    betas, block = args[1].shape[1], args[1].shape[3]
+    chips, cores = lax.axis_size("pair"), lax.axis_size("irrep")
+    fits = lax.axis_size("vtile") == 1 and cores == 2 and betas == 8 and chips == betas * cores
+    if fits and args[8].shape[0] == 2 and block % 2 == 0 and block < LANE:
+        return on_device_scatter(*args)
+    return on_device_gather(*args)
+
+
 def solution(mesh):
     placed = (
         P("pair", None, None),

time: 2050 us -> 602 us (0.29)
  local copies, waits for them, and re-layouts: 817 us -> 94.2 us
  matrix products: 409 us -> 20.4 us
  other arithmetic: 265 us -> 32.3 us
  waiting for transfers between devices: 418 us -> 202 us
  Pallas kernels: 0 us -> 152 us
  loops' own time: 89.9 us -> 0 us
  blocking collectives: 12.6 us -> 59.2 us
  starting transfers between devices: 0.09 us -> 31 us
    add x40 -> x0, local copies, waits for them, and re-layouts: 408 us -> none  [pair_term(): energy_a[:, :, None, None] + beta_energy[:, None, :, None]]
    dot_general x20 -> x8, matrix products: 409 us -> 20.4 us  [the longest x3 17.5 us: on_device_scatter(): arep = jnp.einsum('wgqab,ae->wgbqe', hole, spread)]
    psum x2 -> x0, waiting for transfers between devices: 348 us -> none  [the longest x1 327 us: spread_2(): return lax.psum(jnp.where(mine, shard, jnp.zeros_like(shard)), axis)]
    reshape x30 -> x7, local copies, waits for them, and re-layouts: 290 us -> 19.1 us  [the longest x1 7.32 us: on_device_scatter(): amps = came[source].reshape(kinds, groups, GROUP, rows, block)]
    scatter-add x12 -> x0, other arithmetic: 246 us -> none  [the longest x1 217 us: on_device(): stash = stash.at[row_index, slot].add(spread, mode='drop')]
    ppermute x0 -> x22, waiting for transfers between devices: none -> 155 us  [the longest x12 152 us: across(): return lax.ppermute(x, 'pair', [(t, t ^ bit) for t in range(count)])]
    pallas_call x0 -> x3, Pallas kernels: none -> 152 us  [triples_call(): pl.pallas_call(triples_kernel, grid=grid, in_specs=[pl.BlockSpec(memory_s...]
    another operation x2 -> x0, loops' own time: 89.9 us -> none  [on_device(): lax.map(folded_step, (amplitudes, pair_i, pair_j, stash, seen))]
  transfers between devices with their start and end apart: 3 -> 24, of which waited for: 3 -> 13; matrix products, arithmetic and copies ran while one was open for 15% -> 21% of each run, Pallas kernels for 0% -> 7%
where the time goes in v1:
time: 602 us; the launch traced here: 598 us
  waiting for transfers between devices  202 us (34%)
  Pallas kernels  152 us (25%)
  local copies, waits for them, and re-layouts  94.2 us (16%)
  blocking collectives  59.2 us (10%)
  other arithmetic  32.3 us (5%)
  starting transfers between devices  31 us (5%)
  matrix products  20.4 us (3%)
  between operations  7.37 us (1%)
    ppermute x12, waiting for transfers between devices, across(): return lax.ppermute(x, 'pair', [(t, t ^ bit) for t in range(count)])  152 us
    pallas_call x3, Pallas kernels, triples_call(): pl.pallas_call(triples_kernel, grid=grid, in_specs=[pl.BlockSpec(memory_s...  152 us
    all_gather x1, blocking collectives, on_device_scatter(): lax.all_gather(jnp.stack([pair_i, pair_j]), 'pair', axis=1, tiled=True)  59.2 us
    all_to_all x1, waiting for transfers between devices, on_device_scatter(): lax.all_to_all(total.reshape(chips, local_pairs, share), 'pair', 0, 0, ti...  46.9 us
    unnamed x48, local copies, waits for them, and re-layouts  24.8 us
    dot_general x3, matrix products, on_device_scatter(): arep = jnp.einsum('wgqab,ae->wgbqe', hole, spread)  17.5 us
    ppermute x12, starting transfers between devices, across(): return lax.ppermute(x, 'pair', [(t, t ^ bit) for t in range(count)])  15.4 us
  transfers between devices with their start and end apart: 24, of which 13 were waited for; matrix products, arithmetic and copies ran while one was open for 21% of the time, Pallas kernels for 7%

profile of v1, /device:TPU:12, one launch (start us, length us, event | category | flops | bytes accessed | tf_op | source)
XLA Modules:
  0.0 597.7 jit_solution(13697809118684826135)
XLA Ops:
  0.0 5.6 fusion.83
  5.6 3.1 dynamic-slice_bitcast_fusion
  8.8 1.4 dynamic-slice_bitcast_fusion.1
  15.2 8.0 %gather_fusion.4 = bf16[240,3872]{1,0:T(8,128)(2,1)S(1)} fusion(bf16[5,8,3872]{2,1,0:T(8,128)(2,1)S(1)} %constant_dynamic-slice_fusion.2, s32[240]{0:T(256)S(1)} %reshape.618), kind=kCustom, calls=%fused_computation.4 | custom fusion | bytes 3719040 | tf_op jit(solution)/shard_map/gather | solution.py:297
  23.2 1.7 reshape.575
  24.9 7.2 %all-to-all-start = ((bf16[16,15,3872]{2,1,0:T(8,128)(2,1)}), bf16[16,15,3872]{2,1,0:T(8,128)(2,1)}, u32[]{:S(2)}, u32[]{:S(2)}) async-start(bf16[16,15,3872]{2,1,0:T(8,128)(2,1)} %reshape.575), calls=%async_computation | async-start | bytes 4063232 | tf_op jit(solution)/shard_map/all_to_all | solution.py:299
  32.1 2.1 slice.182
  34.2 1.6 copy-done.10
  35.8 1.3 dynamic-slice_bitcast_fusion.2
  42.1 59.2 %all-gather = s32[16,5,2]{1,2,0:T(2,128)S(1)} all-gather(s32[1,5,2]{1,2,0:T(2,128)S(1)} %add_bitcast_fusion), channel_id=1, replica_groups=mesh['pair'=16,'vtile'=1,'irrep'=2] {'pair'}, dimensions={0}, use_global_device_ids=true | all-gather | bytes 680 | tf_op jit(solution)/shard_map/all_gather | solution.py:282
  101.8 1.2 gather_fusion.6
  103.1 1.2 gather_fusion.7
  104.3 1.2 gather_fusion.10
  105.5 1.2 gather_fusion.9
  114.7 1.9 bitcast_select_fusion.5
  116.6 3.4 collective-permute-start.16
  119.9 3.8 bitcast_select_fusion.1
  124.6 3.8 bitcast_select_fusion.3
  128.3 1.2 collective-permute-start.1
  129.5 24.8 %collective-permute-done.16 = bf16[4,88,2112]{2,1,0:T(8,128)(2,1)S(1)} collective-permute-done((bf16[4,88,2112]{2,1,0:T(8,128)(2,1)S(1)}, bf16[4,88,2112]{2,1,0:T(8,128)(2,1)S(1)}, u32[]{:S(2)}, u32[]{:S(2)}) %collective-permute-start.16) | collective-permute-done | bytes 1486880 | tf_op jit(solution)/shard_map/ppermute | solution.py:215
  155.0 1.3 pad_maximum_fusion.2
  158.3 2.2 reshape.576
  160.4 3.0 gather_fusion.5
  163.4 7.3 %reshape.578 = bf16[3,5,16,44,88]{4,3,2,1,0:T(8,128)(2,1)} reshape(bf16[240,3872]{1,0:T(8,128)(2,1)} %gather_fusion.5) | data formatting | bytes 3717120 | tf_op jit(solution)/shard_map/reshape | solution.py:303
  170.7 4.3 fusion.84
  175.1 4.2 copy.81
  179.3 15.4 %copy.82 = bf16[2,5,16,44,32]{3,2,4,1,0:T(8,128)(2,1)} copy(bf16[2,5,16,44,32]{4,3,2,1,0:T(8,128)(2,1)S(1)} %get-tuple-element.41) | data formatting | bytes 901120
  194.7 6.7 %convolution_bitcast_fusion.1.arep_ref = bf16[2,5,32,16,768]{4,3,2,1,0:T(8,128)(2,1)} fusion(bf16[2,5,16,44,32]{3,2,4,1,0:T(8,128)(2,1)} %copy.81, s32[768]{0:T(1024)S(1)} %add_select_fusion.1, pred[768]{0:T(1024)(128)(4,1)S(1)} %iota_compare_fusion.5), kind=kOutput, calls=%fused_computation.15 | convolution fusion | flops 346097664 | bytes 8318720 | tf_op jit(solution)/shard_map/wgqab,ae->wgbqe/dot_general | solution.py:340
  201.4 5.3 convolution_bitcast_fusion.arep_ref
  206.7 1.9 slice.183
  208.6 2.7 squeeze.203
  211.3 2.4 reshape.577
  213.6 2.2 copy.56
  215.8 2.2 copy.83
  218.0 1.2 pad.8.at_ref
  219.2 5.5 convolution_bitcast_fusion.2.arep_ref
  224.8 2.7 dynamic-slice_select_fusion.3
  227.9 2.1 collective-permute-start.10
  230.0 1.7 collective-permute-done.1
  231.7 2.7 dynamic-slice_select_fusion.11
  235.7 1.5 fusion.27
  237.7 11.3 %collective-permute-done.18 = bf16[2,88,2112]{2,1,0:T(8,128)(2,1)S(1)} collective-permute-done((bf16[2,88,2112]{2,1,0:T(8,128)(2,1)S(1)}, bf16[2,88,2112]{2,1,0:T(8,128)(2,1)S(1)}, u32[]{:S(2)}, u32[]{:S(2)}) %collective-permute-start.18) | collective-permute-done | bytes 743456 | tf_op jit(solution)/shard_map/ppermute | solution.py:215
  249.0 1.5 fusion.31
  250.9 1.5 collective-permute-done.19
  253.6 16.5 %collective-permute-done.20 = bf16[88,2112]{1,0:T(8,128)(2,1)S(1)} collective-permute-done((bf16[88,2112]{1,0:T(8,128)(2,1)S(1)}, bf16[88,2112]{1,0:T(8,128)(2,1)S(1)}, u32[]{:S(2)}, u32[]{:S(2)}) %collective-permute-start.20) | collective-permute-done | bytes 371744 | tf_op jit(solution)/shard_map/ppermute | solution.py:215
  270.2 3.8 collective-permute-done.10
  274.0 26.6 %collective-permute-done.2 = bf16[2,2,88,2816]{3,2,1,0:T(8,128)(2,1)S(1)} collective-permute-done((bf16[2,2,88,2816]{3,2,1,0:T(8,128)(2,1)S(1)}, bf16[2,2,88,2816]{3,2,1,0:T(8,128)(2,1)S(1)}, u32[]{:S(2)}, u32[]{:S(2)}) %collective-permute-start.2) | collective-permute-done | bytes 1982496 | tf_op jit(solution)/shard_map/ppermute | solution.py:215
  301.9 1.7 collective-permute-start.3
  304.3 16.0 %collective-permute-done.11 = bf16[2,88,2816]{2,1,0:T(8,128)(2,1)S(1)} collective-permute-done((bf16[2,88,2816]{2,1,0:T(8,128)(2,1)S(1)}, bf16[2,88,2816]{2,1,0:T(8,128)(2,1)S(1)}, u32[]{:S(2)}, u32[]{:S(2)}) %collective-permute-start.11) | collective-permute-done | bytes 991264 | tf_op jit(solution)/shard_map/ppermute | solution.py:215
  320.3 10.6 %collective-permute-done.3 = bf16[2,88,2816]{2,1,0:T(8,128)(2,1)S(1)} collective-permute-done((bf16[2,88,2816]{2,1,0:T(8,128)(2,1)S(1)}, bf16[2,88,2816]{2,1,0:T(8,128)(2,1)S(1)}, u32[]{:S(2)}, u32[]{:S(2)}) %collective-permute-start.3) | collective-permute-done | bytes 991264 | tf_op jit(solution)/shard_map/ppermute | solution.py:215
  332.0 41.6 %triples.5 = f32[5,768,88]{2,1,0:T(8,128)S(1)} custom-call(f32[2,24]{1,0:T(2,128)S(1)} %slice.139.eb_ref, bf16[2,24,88,128]{3,2,1,0:T(8,128)(2,1)S(1)} %bitcast.228, bf16[2,88,2112]{2,1,0:T(8,128)(2,1)S(1)} %pad_maximum_fusion.5.v_ref, bf16[5,128,768]{2,1,0:T(8,128)(2,1)S(1)} %pad.8.at_ref, bf16[2,5,24,16,768]{4,3,2,1,0:T(8,128)(2,1)} %convolution_bitcast_fusion.2.arep_ref, ...), custom_call_target="tpu_custom_call" | custom-call | flops 11159470080 | bytes 7723008 | tf_op jit(solution)/shard_map/triples/pallas_call | solution.py:177
  374.2 3.2 collective-permute-start.5
  377.5 1.4 collective-permute-start.13
  379.0 31.4 %collective-permute-done.5 = bf16[88,2816]{1,0:T(8,128)(2,1)S(1)} collective-permute-done((bf16[88,2816]{1,0:T(8,128)(2,1)S(1)}, bf16[88,2816]{1,0:T(8,128)(2,1)S(1)}, u32[]{:S(2)}, u32[]{:S(2)}) %collective-permute-start.5) | collective-permute-done | bytes 495648 | tf_op jit(solution)/shard_map/ppermute | solution.py:215
  410.6 9.5 %collective-permute-done.13 = bf16[88,2816]{1,0:T(8,128)(2,1)S(1)} collective-permute-done((bf16[88,2816]{1,0:T(8,128)(2,1)S(1)}, bf16[88,2816]{1,0:T(8,128)(2,1)S(1)}, u32[]{:S(2)}, u32[]{:S(2)}) %collective-permute-start.13) | collective-permute-done | bytes 495648 | tf_op jit(solution)/shard_map/ppermute | solution.py:215
  423.0 54.9 %triples.3 = f32[5,768,88]{2,1,0:T(8,128)} custom-call(f32[2,32]{1,0:T(2,128)S(1)} %get-tuple-element.58.eb_ref, bf16[2,32,88,128]{3,2,1,0:T(8,128)(2,1)S(1)} %bitcast.226, bf16[2,88,2816]{2,1,0:T(8,128)(2,1)S(1)} %pad_maximum_fusion.3.v_ref, bf16[5,128,768]{2,1,0:T(8,128)(2,1)S(1)} %pad.8.at_ref, ...), custom_call_target="tpu_custom_call" | custom-call | flops 14879293440 | bytes 10297344 | tf_op jit(solution)/shard_map/triples/pallas_call | solution.py:177
  477.9 55.1 %triples.4 = f32[5,768,88]{2,1,0:T(8,128)} custom-call(f32[2,32]{1,0:T(2,128)S(1)} %get-tuple-element.59.eb_ref, bf16[2,32,88,128]{3,2,1,0:T(8,128)(2,1)S(1)} %bitcast.227, bf16[2,88,2816]{2,1,0:T(8,128)(2,1)S(1)} %pad_maximum_fusion.4.v_ref, bf16[5,128,768]{2,1,0:T(8,128)(2,1)S(1)} %pad.8.at_ref, ...), custom_call_target="tpu_custom_call" | custom-call | flops 14879293440 | bytes 10297344 | tf_op jit(solution)/shard_map/triples/pallas_call | solution.py:177
  533.0 3.2 slice_add_fusion
  536.2 1.9 reshape.583
  538.1 1.0 gather_fusion.12
  539.1 1.5 reshape.584
  540.7 7.0 %all-to-all-start.1 = ((f32[16,5,3872]{2,1,0:T(8,128)}), f32[16,5,3872]{2,1,0:T(8,128)S(1)}, u32[]{:S(2)}, u32[]{:S(2)}) async-start(f32[16,5,3872]{2,1,0:T(8,128)} %reshape.584), calls=%async_computation.1 | async-start | bytes 4063232 | tf_op jit(solution)/shard_map/all_to_all | solution.py:344
  547.8 46.9 %all-to-all-done.1 = f32[16,5,3872]{2,1,0:T(8,128)S(1)} async-done(((f32[16,5,3872]{2,1,0:T(8,128)}), f32[16,5,3872]{2,1,0:T(8,128)S(1)}, u32[]{:S(2)}, u32[]{:S(2)}) %all-to-all-start.1) | async-done | bytes 1239072 | tf_op jit(solution)/shard_map/all_to_all | solution.py:344
  595.1 2.4 gather_fusion.13
  (197 shorter events, 26.4 us)
Async XLA Ops:
  0.0 15.1 %copy-start = (bf16[5,8,7744]{2,1,0:T(8,128)(2,1)S(1)}, bf16[5,8,7744]{2,1,0:T(8,128)(2,1)}, u32[]{:S(2)}) copy-start(bf16[5,8,7744]{2,1,0:T(8,128)(2,1)} %param.10) | copy-start | bytes 1858564
  5.6 3.2 copy-start.7
  8.8 111.2 %collective-permute-start.8 = (bf16[4,88,2816]{2,1,0:T(8,128)(2,1)}, bf16[4,88,2816]{2,1,0:T(8,128)(2,1)}, u32[]{:S(2)}, u32[]{:S(2)}) collective-permute-start(bf16[4,88,2816]{2,1,0:T(8,128)(2,1)} %dynamic-slice_bitcast_fusion), channel_id=1, source_target_pairs={{0,1},{1,0},{2,3},{3,2},{4,5},{5,4},{6,7},{7,6},{8,9},{9,8},{10,11... | collective-permute-start | bytes 5947400 | tf_op jit(solution)/shard_map/ppermute | solution.py:210
  8.8 2.0 copy-start.16
  8.8 2.0 copy-start.21
  8.8 2.0 copy-start.2
  8.8 2.7 copy-start.18
  8.8 4.7 copy-start.19
  8.8 4.7 copy-start.20
  10.3 114.3 %collective-permute-start = (bf16[4,88,2816]{2,1,0:T(8,128)(2,1)}, bf16[4,88,2816]{2,1,0:T(8,128)(2,1)}, u32[]{:S(2)}, u32[]{:S(2)}) collective-permute-start(bf16[4,88,2816]{2,1,0:T(8,128)(2,1)} %dynamic-slice_bitcast_fusion.1), channel_id=1, source_target_pairs={{0,1},{1,0},{2,3},{3,2},{4,5},{5,4},{6,7},{7,6},{8,9},{9,8},{10,11... | collective-permute-start | bytes 5947400 | tf_op jit(solution)/shard_map/ppermute | solution.py:210
  10.7 101.2 %collective-permute-start.7 = (bf16[2,30,30,88]{3,0,2,1:T(2,128)(2,1)S(1)}, bf16[2,30,30,88]{3,0,2,1:T(2,128)(2,1)}, u32[]{:S(2)}, u32[]{:S(2)}) collective-permute-start(bf16[2,30,30,88]{3,0,2,1:T(2,128)(2,1)S(1)} %copy-done.16), channel_id=1, source_target_pairs={{0,1},{1,0},{2,3},{3,2},{4,5},{5,4},{6,7},{7,6},{8,9},{9,8},{10,11... | collective-permute-start | bytes 950408 | tf_op jit(solution)/shard_map/ppermute | solution.py:210
  24.9 133.4 %all-to-all-start = ((bf16[16,15,3872]{2,1,0:T(8,128)(2,1)}), bf16[16,15,3872]{2,1,0:T(8,128)(2,1)}, u32[]{:S(2)}, u32[]{:S(2)}) async-start(bf16[16,15,3872]{2,1,0:T(8,128)(2,1)} %reshape.575), calls=%async_computation | async-start | bytes 4063232 | tf_op jit(solution)/shard_map/all_to_all | solution.py:299
  34.1 1.6 copy-start.10
  35.8 68.5 %copy-start.3 = (f32[30]{0:T(128)S(1)}, f32[30]{0:T(128)}, u32[]{:S(2)}) copy-start(f32[30]{0:T(128)} %param.13) | copy-start | bytes 364
  37.1 70.4 %copy-start.17 = (f32[8,88]{1,0:T(8,128)S(1)}, f32[8,88]{1,0:T(8,128)}, u32[]{:S(2)}) copy-start(f32[8,88]{1,0:T(8,128)} %param.14) | copy-start | bytes 8452
  37.1 77.6 %collective-permute-start.15 = (bf16[4,88,2112]{2,1,0:T(8,128)(2,1)}, bf16[4,88,2112]{2,1,0:T(8,128)(2,1)S(1)}, u32[]{:S(2)}, u32[]{:S(2)}) collective-permute-start(bf16[4,88,2112]{2,1,0:T(8,128)(2,1)} %dynamic-slice_bitcast_fusion.2), channel_id=1, source_target_pairs={{0,1},{1,0},{2,3},{3,2},{4,5},{5,4},{6,7},{7,6},{8,9},{9,8},{10,11... | collective-permute-start | bytes 4460552 | tf_op jit(solution)/shard_map/ppermute | solution.py:210
  114.6 5.3 copy-start.9
  116.6 8.0 %copy-start.8 = (bf16[8,88,2816]{2,1,0:T(8,128)(2,1)S(1)}, bf16[8,88,2816]{2,1,0:T(8,128)(2,1)}, u32[]{:S(2)}) copy-start(bf16[8,88,2816]{2,1,0:T(8,128)(2,1)} %get-tuple-element.8) | copy-start | bytes 11894788
  116.6 37.7 %collective-permute-start.16 = (bf16[4,88,2112]{2,1,0:T(8,128)(2,1)S(1)}, bf16[4,88,2112]{2,1,0:T(8,128)(2,1)S(1)}, u32[]{:S(2)}, u32[]{:S(2)}) collective-permute-start(bf16[4,88,2112]{2,1,0:T(8,128)(2,1)S(1)} %get-tuple-element.15), channel_id=1, source_target_pairs={{0,2},{2,0},{4,6},{6,4},{8,10},{10,8},{12,14},{14,12},{16,18},{18,... | collective-permute-start | bytes 4460552 | tf_op jit(solution)/shard_map/ppermute | solution.py:215
  123.7 101.1 %collective-permute-start.9 = (bf16[4,88,2816]{2,1,0:T(8,128)(2,1)}, bf16[4,88,2816]{2,1,0:T(8,128)(2,1)}, u32[]{:S(2)}, u32[]{:S(2)}) collective-permute-start(bf16[4,88,2816]{2,1,0:T(8,128)(2,1)} %get-tuple-element.13), channel_id=1, source_target_pairs={{0,2},{2,0},{4,6},{6,4},{8,10},{10,8},{12,14},{14,12},{16,18},{18,... | collective-permute-start | bytes 5947400 | tf_op jit(solution)/shard_map/ppermute | solution.py:215
  128.3 103.3 %collective-permute-start.1 = (bf16[4,88,2816]{2,1,0:T(8,128)(2,1)}, bf16[4,88,2816]{2,1,0:T(8,128)(2,1)}, u32[]{:S(2)}, u32[]{:S(2)}) collective-permute-start(bf16[4,88,2816]{2,1,0:T(8,128)(2,1)} %get-tuple-element.11), channel_id=1, source_target_pairs={{0,2},{2,0},{4,6},{6,4},{8,10},{10,8},{12,14},{14,12},{16,18},{18,... | collective-permute-start | bytes 5947400 | tf_op jit(solution)/shard_map/ppermute | solution.py:215
  156.3 78.1 %collective-permute-start.17 = (bf16[2,2,88,2112]{3,2,1,0:T(8,128)(2,1)}, bf16[2,2,88,2112]{3,2,1,0:T(8,128)(2,1)}, u32[]{:S(2)}, u32[]{:S(2)}) collective-permute-start(bf16[2,2,88,2112]{3,2,1,0:T(8,128)(2,1)} %pad_maximum_fusion.2), channel_id=1, source_target_pairs={{0,4},{2,6},{4,0},{6,2},{8,12},{10,14},{12,8},{14,10},{16,20},{18,... | collective-permute-start | bytes 4460552 | tf_op jit(solution)/shard_map/ppermute | solution.py:215
  194.7 6.7 %copy-start.15 = (bf16[2,5,16,44,32]{3,2,4,1,0:T(8,128)(2,1)S(1)}, bf16[2,5,16,44,32]{3,2,4,1,0:T(8,128)(2,1)}, u32[]{:S(2)}) copy-start(bf16[2,5,16,44,32]{3,2,4,1,0:T(8,128)(2,1)} %copy.82) | copy-start | bytes 1351684
  201.4 5.3 copy-start.4
  206.7 1.9 slice-start
  211.3 4.6 copy-start.11
  219.2 5.6 copy-start.6
  227.7 4.0 copy-start.5
  227.9 46.1 %collective-permute-start.10 = (bf16[2,2,88,2816]{3,2,1,0:T(8,128)(2,1)S(1)}, bf16[2,2,88,2816]{3,2,1,0:T(8,128)(2,1)S(1)}, u32[]{:S(2)}, u32[]{:S(2)}) collective-permute-start(bf16[2,2,88,2816]{3,2,1,0:T(8,128)(2,1)S(1)} %pad_maximum_fusion.1), channel_id=1, source_target_pairs={{0,4},{2,6},{4,0},{6,2},{8,12},{10,14},{12,8},{14,10},{16,20},{18,... | collective-permute-start | bytes 5947400 | tf_op jit(solution)/shard_map/ppermute | solution.py:215
  234.3 1.1 copy-start.12
  234.4 1.3 copy-start.13
  237.2 11.8 %collective-permute-start.18 = (bf16[2,88,2112]{2,1,0:T(8,128)(2,1)S(1)}, bf16[2,88,2112]{2,1,0:T(8,128)(2,1)S(1)}, u32[]{:S(2)}, u32[]{:S(2)}) collective-permute-start(bf16[2,88,2112]{2,1,0:T(8,128)(2,1)S(1)} %fusion.27), channel_id=1, source_target_pairs={{0,8},{2,10},{4,12},{6,14},{8,0},{10,2},{12,4},{14,6},{16,24},{18,... | collective-permute-start | bytes 2230280 | tf_op jit(solution)/shard_map/ppermute | solution.py:215
  237.6 63.1 %collective-permute-start.2 = (bf16[2,2,88,2816]{3,2,1,0:T(8,128)(2,1)S(1)}, bf16[2,2,88,2816]{3,2,1,0:T(8,128)(2,1)S(1)}, u32[]{:S(2)}, u32[]{:S(2)}) collective-permute-start(bf16[2,2,88,2816]{3,2,1,0:T(8,128)(2,1)S(1)} %pad_maximum_fusion), channel_id=1, source_target_pairs={{0,4},{2,6},{4,0},{6,2},{8,12},{10,14},{12,8},{14,10},{16,20},{18,... | collective-permute-start | bytes 5947400 | tf_op jit(solution)/shard_map/ppermute | solution.py:215
  250.6 1.8 collective-permute-start.19
  252.4 17.6 %collective-permute-start.20 = (bf16[88,2112]{1,0:T(8,128)(2,1)S(1)}, bf16[88,2112]{1,0:T(8,128)(2,1)S(1)}, u32[]{:S(2)}, u32[]{:S(2)}) collective-permute-start(bf16[88,2112]{1,0:T(8,128)(2,1)S(1)} %bitcast_select_fusion.10), channel_id=1, source_target_pairs={{0,16},{2,18},{4,20},{6,22},{8,24},{10,26},{12,28},{14,30},{16,0},... | collective-permute-start | bytes 1115144 | tf_op jit(solution)/shard_map/ppermute | solution.py:215
  270.1 33.5 %collective-permute-start.21 = (bf16[88,2112]{1,0:T(8,128)(2,1)S(1)}, bf16[88,2112]{1,0:T(8,128)(2,1)S(1)}, u32[]{:S(2)}, u32[]{:S(2)}) collective-permute-start(bf16[88,2112]{1,0:T(8,128)(2,1)S(1)} %fusion.37), channel_id=1, source_target_pairs={{0,1},{1,0},{2,3},{3,2},{4,5},{5,4},{6,7},{7,6},{8,9},{9,8},{10,11... | collective-permute-start | bytes 1115144 | tf_op jit(solution)/shard_map/ppermute | solution.py:210
  301.5 18.8 %collective-permute-start.11 = (bf16[2,88,2816]{2,1,0:T(8,128)(2,1)S(1)}, bf16[2,88,2816]{2,1,0:T(8,128)(2,1)S(1)}, u32[]{:S(2)}, u32[]{:S(2)}) collective-permute-start(bf16[2,88,2816]{2,1,0:T(8,128)(2,1)S(1)} %get-tuple-element.63), channel_id=1, source_target_pairs={{0,8},{2,10},{4,12},{6,14},{8,0},{10,2},{12,4},{14,6},{16,24},{18,... | collective-permute-start | bytes 2973704 | tf_op jit(solution)/shard_map/ppermute | solution.py:215
  301.9 29.0 %collective-permute-start.3 = (bf16[2,88,2816]{2,1,0:T(8,128)(2,1)S(1)}, bf16[2,88,2816]{2,1,0:T(8,128)(2,1)S(1)}, u32[]{:S(2)}, u32[]{:S(2)}) collective-permute-start(bf16[2,88,2816]{2,1,0:T(8,128)(2,1)S(1)} %get-tuple-element.62), channel_id=1, source_target_pairs={{0,8},{2,10},{4,12},{6,14},{8,0},{10,2},{12,4},{14,6},{16,24},{18,... | collective-permute-start | bytes 2973704 | tf_op jit(solution)/shard_map/ppermute | solution.py:215
  331.8 42.4 %collective-permute-start.4 = (bf16[88,2816]{1,0:T(8,128)(2,1)S(1)}, bf16[88,2816]{1,0:T(8,128)(2,1)S(1)}, u32[]{:S(2)}, u32[]{:S(2)}) collective-permute-start(bf16[88,2816]{1,0:T(8,128)(2,1)S(1)} %dynamic-slice_bitcast_fusion.4), channel_id=1, source_target_pairs={{0,1},{1,0},{2,3},{3,2},{4,5},{5,4},{6,7},{7,6},{8,9},{9,8},{10,11... | collective-permute-start | bytes 1486856 | tf_op jit(solution)/shard_map/ppermute | solution.py:210
  373.6 3.9 collective-permute-start.12
  374.2 36.2 %collective-permute-start.5 = (bf16[88,2816]{1,0:T(8,128)(2,1)S(1)}, bf16[88,2816]{1,0:T(8,128)(2,1)S(1)}, u32[]{:S(2)}, u32[]{:S(2)}) collective-permute-start(bf16[88,2816]{1,0:T(8,128)(2,1)S(1)} %bitcast_select_fusion.8), channel_id=1, source_target_pairs={{0,16},{2,18},{4,20},{6,22},{8,24},{10,26},{12,28},{14,30},{16,0},... | collective-permute-start | bytes 1486856 | tf_op jit(solution)/shard_map/ppermute | solution.py:215
  377.5 42.6 %collective-permute-start.13 = (bf16[88,2816]{1,0:T(8,128)(2,1)S(1)}, bf16[88,2816]{1,0:T(8,128)(2,1)S(1)}, u32[]{:S(2)}, u32[]{:S(2)}) collective-permute-start(bf16[88,2816]{1,0:T(8,128)(2,1)S(1)} %bitcast_select_fusion.6), channel_id=1, source_target_pairs={{0,16},{2,18},{4,20},{6,22},{8,24},{10,26},{12,28},{14,30},{16,0},... | collective-permute-start | bytes 1486856 | tf_op jit(solution)/shard_map/ppermute | solution.py:215
  410.5 9.7 %collective-permute-start.6 = (bf16[88,2816]{1,0:T(8,128)(2,1)S(1)}, bf16[88,2816]{1,0:T(8,128)(2,1)S(1)}, u32[]{:S(2)}, u32[]{:S(2)}) collective-permute-start(bf16[88,2816]{1,0:T(8,128)(2,1)S(1)} %fusion.34), channel_id=1, source_target_pairs={{0,1},{1,0},{2,3},{3,2},{4,5},{5,4},{6,7},{7,6},{8,9},{9,8},{10,11... | collective-permute-start | bytes 1486856 | tf_op jit(solution)/shard_map/ppermute | solution.py:210
  420.2 1.9 collective-permute-start.14
  477.9 55.1 %copy-start.14 = (f32[5,768,88]{2,1,0:T(8,128)S(1)}, f32[5,768,88]{2,1,0:T(8,128)}, u32[]{:S(2)}) copy-start(f32[5,768,88]{2,1,0:T(8,128)} %triples.3) | copy-start | bytes 4055044
  540.7 54.1 %all-to-all-start.1 = ((f32[16,5,3872]{2,1,0:T(8,128)}), f32[16,5,3872]{2,1,0:T(8,128)S(1)}, u32[]{:S(2)}, u32[]{:S(2)}) async-start(f32[16,5,3872]{2,1,0:T(8,128)} %reshape.584), calls=%async_computation.1 | async-start | bytes 4063232 | tf_op jit(solution)/shard_map/all_to_all | solution.py:344
  594.9 2.6 copy-start.1

commit v2 on v1

--- a/solution.py
+++ b/solution.py
@@ -1,3 +1,4 @@
+import functools
 import math
 
 import jax
@@ -128,13 +129,12 @@
     return [(first, min(size, block - first)) for first in range(0, block, size)]
 
 
-def triples_kernel(
-    eb_ref, vt_ref, v_ref, at_ref, arep_ref, ct_ref, mask_ref, ecol_ref, lrow_ref, o_ref, t_ref, acc_ref
-):
+def triples_kernel(last, *refs):
+    eb_ref, vt_ref, v_ref, at_ref, arep_ref, ct_ref, mask_ref, ecol_ref, lrow_ref = refs[:9]
+    o_ref, t_ref = refs[-2:]
     count, block = vt_ref.shape[1], vt_ref.shape[2]
     depth = mask_ref.shape[1] // GROUP
     tiles = mask_ref.shape[0]
-    window = pl.program_id(1)
 
     def pair_of_b(step, carry):
         for tile in range(tiles):
@@ -148,62 +148,66 @@
                 bottom = jnp.concatenate([hole_amp] * depth, axis=0) * mask_ref[tile]
                 rhs = jnp.concatenate([top, bottom], axis=0)
                 numer = jnp.dot(lhs, rhs, preferred_element_type=jnp.float32)
-                denom = (ecol_ref[...] + eb_ref[window, b]) + lrow_ref[0, 0, :, lanes]
+                denom = (ecol_ref[...] + eb_ref[0, b]) + lrow_ref[0, 0, :, lanes]
                 results.append(numer / denom)
             rows = pl.ds(pl.multiple_of(step * (2 * block), 2 * block), 2 * block)
             t_ref[rows, lanes] = jnp.concatenate(results, axis=0).astype(jnp.bfloat16)
         return carry
 
     lax.fori_loop(0, count // 2, pair_of_b, 0)
-    contrib = jnp.dot(v_ref[0], t_ref[...], preferred_element_type=jnp.float32)
-
-    @pl.when(window == 0)
-    def _():
-        acc_ref[...] = contrib
-
-    @pl.when(window > 0)
-    def _():
-        acc_ref[...] += contrib
-
-    @pl.when(window == pl.num_programs(1) - 1)
-    def _():
-        o_ref[0] = acc_ref[...].T
-
-
-def triples_call(eb, vt, v, at, arep, ct, mask, ecol, lrow):
-    windows, count, block, _ = vt.shape
+
+    def finish(tile, carry):
+        lanes = pl.ds(pl.multiple_of(tile * TILE, TILE), TILE)
+        contrib = jnp.dot(v_ref[0], t_ref[:, lanes], preferred_element_type=jnp.float32)
+        if len(refs) == 12:
+            contrib = contrib + refs[9][0, :, lanes]
+        if last:
+            o_ref[0, lanes, :] = contrib.T
+        else:
+            o_ref[0, :, lanes] = contrib
+        return carry
+
+    lax.fori_loop(0, tiles, finish, 0)
+
+
+def triples_call(window, last, eb, vt, v, at, arep, ct, mask, ecol, lrow, total=None):
+    _, count, block, _ = vt.shape
     groups, depth_rows, lanes = at.shape
-    grid = (groups, windows)
+    w = window
+    tall, wide = pl.BlockSpec((1, lanes, block), lambda g: (g, 0, 0)), pl.BlockSpec((1, block, lanes), lambda g: (g, 0, 0))
+    in_specs = [
+        pl.BlockSpec(memory_space=pltpu.SMEM),
+        pl.BlockSpec((1, count, block, LANE), lambda g: (w, 0, 0, 0)),
+        pl.BlockSpec((1, block, count * block), lambda g: (w, 0, 0)),
+        pl.BlockSpec((1, depth_rows, lanes), lambda g: (g, 0, 0)),
+        pl.BlockSpec((1, 1, count, GROUP, lanes), lambda g: (w, g, 0, 0, 0)),
+        pl.BlockSpec((1, 1) + ct.shape[2:], lambda g: (w, g, 0, 0, 0)),
+        pl.BlockSpec(mask.shape, lambda g: (0, 0, 0)),
+        pl.BlockSpec(ecol.shape, lambda g: (0, 0)),
+        pl.BlockSpec((1, 1, 1, lanes), lambda g: (w, g, 0, 0)),
+    ]
+    operands = [eb[w : w + 1], vt, v, at, arep, ct, mask, ecol, lrow]
+    if total is not None:
+        in_specs.append(wide)
+        operands.append(total)
+    shape = (groups, lanes, block) if last else (groups, block, lanes)
     return pl.pallas_call(
-        triples_kernel,
-        grid=grid,
-        in_specs=[
-            pl.BlockSpec(memory_space=pltpu.SMEM),
-            pl.BlockSpec((1, count, block, LANE), lambda g, w: (w, 0, 0, 0)),
-            pl.BlockSpec((1, block, count * block), lambda g, w: (w, 0, 0)),
-            pl.BlockSpec((1, depth_rows, lanes), lambda g, w: (g, 0, 0)),
-            pl.BlockSpec((1, 1, count, GROUP, lanes), lambda g, w: (w, g, 0, 0, 0)),
-            pl.BlockSpec((1, 1) + ct.shape[2:], lambda g, w: (w, g, 0, 0, 0)),
-            pl.BlockSpec(mask.shape, lambda g, w: (0, 0, 0)),
-            pl.BlockSpec(ecol.shape, lambda g, w: (0, 0)),
-            pl.BlockSpec((1, 1, 1, lanes), lambda g, w: (w, g, 0, 0)),
-        ],
-        out_specs=pl.BlockSpec((1, lanes, block), lambda g, w: (g, 0, 0)),
-        out_shape=jax.ShapeDtypeStruct((groups, lanes, block), jnp.float32),
-        scratch_shapes=[
-            pltpu.VMEM((count * block, lanes), jnp.bfloat16),
-            pltpu.VMEM((block, lanes), jnp.float32),
-        ],
+        functools.partial(triples_kernel, last),
+        grid=(groups,),
+        in_specs=in_specs,
+        out_specs=tall if last else wide,
+        out_shape=jax.ShapeDtypeStruct(shape, jnp.float32),
+        scratch_shapes=[pltpu.VMEM((count * block, lanes), jnp.bfloat16)],
         compiler_params=pltpu.CompilerParams(
-            dimension_semantics=("arbitrary", "arbitrary"), vmem_limit_bytes=48 * 1024 * 1024
+            dimension_semantics=("arbitrary",), vmem_limit_bytes=40 * 1024 * 1024
         ),
         cost_estimate=pl.CostEstimate(
-            flops=groups * windows * count * block * lanes * 2 * (TILE + block),
-            bytes_accessed=arep.size * 2 + vt.size * 2 + v.size * 2,
-            transcendentals=groups * windows * count * block * lanes,
+            flops=groups * count * block * lanes * 2 * (TILE + block) * 4,
+            bytes_accessed=(arep.size + vt.size + v.size) * 2,
+            transcendentals=groups * count * block * lanes,
         ),
         name="triples",
-    )(eb, vt, v, at, arep, ct, mask, ecol, lrow)
+    )(*operands)
 
 
 def swap_cores(x):
@@ -219,40 +223,55 @@
     return lax.dynamic_index_in_dim(x, index, 0, keepdims=False)
 
 
-def fetch_slab(slab, owner, k_irrep, me, core):
-    windows = owner.shape[0]
-    bits = [(me >> n) & 1 for n in range(4)]
-    gamma = bits[0]
-    owner_bits = [[(owner[w] >> n) & 1 for n in range(4)] for w in range(windows)]
-    halves = slab.reshape((2, slab.shape[0] // 2) + slab.shape[1:])
-    mine, theirs = pick(halves, core), swap_cores(pick(halves, 1 - core))
-    same = gamma == core
-    here = jnp.where(same, mine, theirs)
-    there = across(jnp.where(same, theirs, mine), 1)
-
-    def low_block(w, high, low):
-        beta = (2 * high + low) ^ (k_irrep[w] & 3) ^ gamma
-        return jnp.where(owner_bits[w][0] == bits[0], pick(here, beta), pick(there, beta))
-
-    def low_blocks(low):
-        return jnp.stack([jnp.stack([low_block(w, high, low) for w in range(windows)]) for high in range(2)])
-
-    kept = low_blocks(bits[1])
-    came = across(low_blocks(1 - bits[1]), 2)
-    from_here = jnp.stack([owner_bits[w][1] == bits[1] for w in range(windows)])[:, None, None]
-    keep2 = jnp.where(from_here, pick(kept, bits[2]), pick(came, bits[2]))
-    send2 = jnp.where(from_here, pick(kept, 1 - bits[2]), pick(came, 1 - bits[2]))
-    came = across(send2, 4)
-    from_here = jnp.stack([owner_bits[w][2] == bits[2] for w in range(windows)])[:, None, None]
-    blocks = jnp.where(from_here, keep2, came)
-    mine, theirs = pick(blocks, core), swap_cores(pick(blocks, 1 - core))
-    high = (k_irrep[core] >> 2) & 1
-    mine_stays = (bits[3] ^ high) == core
-    kept = jnp.where(mine_stays, mine, theirs)
-    came = across(jnp.where(mine_stays, theirs, mine), 8)
-    block = jnp.where(((owner[core] >> 3) & 1) == bits[3], kept, came)
-    other = swap_cores(block)
-    return jnp.stack([jnp.where(core == 0, block, other), jnp.where(core == 0, other, block)])
+def after(x, *others):
+    return lax.optimization_barrier((x,) + others)[0]
+
+
+class SlabPath:
+    def __init__(self, owner, k_irrep, me, core):
+        self.owner, self.k_irrep, self.core = owner, k_irrep, core
+        self.windows = owner.shape[0]
+        self.bits = [(me >> n) & 1 for n in range(4)]
+
+    def from_here(self, bit):
+        return ((self.owner >> bit) & 1) == self.bits[bit]
+
+    def split_cores(self, slab):
+        halves = slab.reshape((2, slab.shape[0] // 2) + slab.shape[1:])
+        mine, theirs = pick(halves, self.core), swap_cores(pick(halves, 1 - self.core))
+        same = self.bits[0] == self.core
+        return jnp.where(same, mine, theirs), jnp.where(same, theirs, mine)
+
+    def split_low(self, kept, came):
+        def block(w, high, low):
+            beta = (2 * high + low) ^ (self.k_irrep[w] & 3) ^ self.bits[0]
+            return jnp.where(self.from_here(0)[w], pick(kept, beta), pick(came, beta))
+
+        def blocks(low):
+            return jnp.stack(
+                [jnp.stack([block(w, high, low) for w in range(self.windows)]) for high in range(2)]
+            )
+
+        return blocks(self.bits[1]), blocks(1 - self.bits[1])
+
+    def split_high(self, kept, came):
+        here = self.from_here(1)[:, None, None]
+        kept, leaving = [
+            jnp.where(here, pick(kept, high), pick(came, high)) for high in (self.bits[2], 1 - self.bits[2])
+        ]
+        return kept, leaving
+
+    def split_top(self, kept, came):
+        blocks = jnp.where(self.from_here(2)[:, None, None], kept, came)
+        mine, theirs = pick(blocks, self.core), swap_cores(pick(blocks, 1 - self.core))
+        stays = (self.bits[3] ^ ((self.k_irrep[self.core] >> 2) & 1)) == self.core
+        return jnp.where(stays, mine, theirs), jnp.where(stays, theirs, mine)
+
+    def join(self, kept, came):
+        block = jnp.where(self.from_here(3)[self.core], kept, came)
+        other = swap_cores(block)
+        first = self.core == 0
+        return jnp.stack([jnp.where(first, block, other), jnp.where(first, other, block)])
 
 
 def on_device_scatter(
@@ -274,12 +293,32 @@
 
     chunks = b_chunks(block)
     local = slabs[0, :, 0]
-    pieces = [
-        fetch_slab(local[:, :, first * block : (first + size) * block], owner, k_irrep, me, core)
-        for first, size in chunks
-    ]
-
-    both = lax.all_gather(jnp.stack([pair_i, pair_j]), "pair", axis=1, tiled=True)
+    path = SlabPath(owner, k_irrep, me, core)
+    kept_x, sent_x = zip(
+        *[path.split_cores(local[:, :, first * block : (first + size) * block]) for first, size in chunks]
+    )
+    x = []
+    for leaving in sent_x:
+        x.append(across(after(leaving, x[-1]) if x else leaving, 1))
+    kept_y, sent_y = [list(v) for v in zip(*map(path.split_low, kept_x, x))]
+    y = [across(leaving, 2) for leaving in sent_y]
+
+    pair_sym = occ_irrep[pair_i] ^ occ_irrep[pair_j]
+    mine = lax.dynamic_slice_in_dim(amplitudes, core * share, share, 2)
+    target = jnp.arange(chips, dtype=jnp.int32)
+    wanted = jnp.stack([target >> 1] + [(target >> 1) ^ (target & 1) ^ k_irrep[w] for w in range(windows)], 1)
+    index = wanted[:, :, None] ^ pair_sym[None, None, :]
+    sent = mine[jnp.arange(local_pairs, dtype=jnp.int32)[None, None, :], index]
+    kinds = 1 + windows
+    sent = sent.reshape(chips, kinds * local_pairs, share)
+    labels = jnp.concatenate([pair_i, pair_j]).astype(bf16)
+    labels = jnp.pad(labels, (0, share - labels.shape[0]))
+    sent = jnp.concatenate([sent, jnp.broadcast_to(labels, (chips, 1, share))], 1)
+    came = lax.all_to_all(after(sent, sent_x[0]), "pair", 0, 0, tiled=True)
+    came = after(came, sent_y[0])
+    both = came[:, -1, : 2 * local_pairs].astype(jnp.int32).reshape(chips, 2, local_pairs)
+    both = both.transpose(1, 0, 2).reshape(2, pairs)
+
     numbers = jnp.arange(pairs, dtype=jnp.int32)
     ahead = both[0][None, :] < both[0][:, None]
     tied = (both[0][None, :] == both[0][:, None]) & (numbers[None, :] < numbers[:, None])
@@ -289,16 +328,8 @@
     first = jnp.sum(placed * both[0][None, :], axis=1)
     second = jnp.sum(placed * both[1][None, :], axis=1)
 
-    pair_sym = occ_irrep[pair_i] ^ occ_irrep[pair_j]
-    mine = lax.dynamic_slice_in_dim(amplitudes, core * share, share, 2)
-    target = jnp.arange(chips, dtype=jnp.int32)
-    wanted = jnp.stack([target >> 1] + [(target >> 1) ^ (target & 1) ^ k_irrep[w] for w in range(windows)], 1)
-    index = wanted[:, :, None] ^ pair_sym[None, None, :]
-    sent = mine[jnp.arange(local_pairs, dtype=jnp.int32)[None, None, :], index]
-    kinds = 1 + windows
-    came = lax.all_to_all(sent.reshape(chips, kinds * local_pairs, share), "pair", 0, 0, tiled=True)
-    came = came.reshape(chips * kinds * local_pairs, share)
-    source = (order // local_pairs) * (kinds * local_pairs) + order % local_pairs
+    came = came.reshape(chips * (kinds * local_pairs + 1), share)
+    source = (order // local_pairs) * (kinds * local_pairs + 1) + order % local_pairs
     source = source[None, :] + local_pairs * jnp.arange(kinds, dtype=jnp.int32)[:, None]
     amps = came[source].reshape(kinds, groups, GROUP, rows, block)
     used = GROUP * rows
@@ -333,13 +364,48 @@
     energy_b = vir_energy[m ^ gamma ^ k_irrep]
 
     eye = (jnp.arange(block)[:, None] == jnp.arange(LANE)[None, :]).astype(bf16)
+    areps = [
+        jnp.einsum("wgqab,ae->wgbqe", amps[1:, :, :, :, start : start + size], spread) for start, size in chunks
+    ]
+
+    def run(chunk, w, v, total):
+        start, size = chunks[chunk]
+        vt = jnp.einsum("wdx,de->wxe", v, eye).reshape(windows, size, block, LANE)
+        last = start + size == block and w == windows - 1
+        energies = energy_b[:, start : start + size]
+        return triples_call(w, last, energies, vt, v, at, areps[chunk], ct, mask, ecol, lrow, total)
+
+    calls = [(chunk, w) for chunk in range(len(chunks)) for w in range(windows)]
+    kept_z, sent_z, kept_h, sent_h, z, h, ready = {}, {}, {}, {}, {}, {}, {}
+
+    def to_high(chunk, token=None):
+        came_y = y[chunk] if token is None else after(y[chunk], token)
+        kept_z[chunk], sent_z[chunk] = path.split_high(kept_y[chunk], came_y)
+        z[chunk] = across(sent_z[chunk], 4)
+        return sent_z[chunk]
+
+    def to_top(chunk, token=None):
+        came_z = z[chunk] if token is None else after(z[chunk], token)
+        kept_h[chunk], sent_h[chunk] = path.split_top(kept_z[chunk], came_z)
+        h[chunk] = across(sent_h[chunk], 8)
+        return sent_h[chunk]
+
+    def arrive(chunk, token=None):
+        came_h = h[chunk] if token is None else after(h[chunk], token)
+        ready[chunk] = path.join(kept_h[chunk], came_h)
+        return ready[chunk]
+
+    plan = {0: [(to_top, 1), (to_high, 2)], 1: [(arrive, 1), (to_top, 2)], 2: [(arrive, 2)]}
+    to_high(0)
+    to_top(0)
+    arrive(0)
+    ready[0] = after(ready[0], to_high(1), sent_y[2])
     total = None
-    for (start, size), v in zip(chunks, pieces):
-        vt = jnp.einsum("wdx,de->wxe", v, eye).reshape(windows, size, block, LANE)
-        hole = amps[1:, :, :, :, start : start + size]
-        arep = jnp.einsum("wgqab,ae->wgbqe", hole, spread)
-        part = triples_call(energy_b[:, start : start + size], vt, v, at, arep, ct, mask, ecol, lrow)
-        total = part if total is None else total + part
+    for n, (chunk, w) in enumerate(calls):
+        total = run(chunk, w, ready[chunk], total)
+        issued = [move(number, total) for move, number in plan.get(n, [])]
+        if issued:
+            total = after(total, *issued)
     total = total[:, :used].reshape(pairs, share)[rank]
     came = lax.all_to_all(total.reshape(chips, local_pairs, share), "pair", 0, 0, tiled=True)
     came = came.reshape(betas, 2, local_pairs, share)
@@ -352,7 +418,8 @@
     betas, block = args[1].shape[1], args[1].shape[3]
     chips, cores = lax.axis_size("pair"), lax.axis_size("irrep")
     fits = lax.axis_size("vtile") == 1 and cores == 2 and betas == 8 and chips == betas * cores
-    if fits and args[8].shape[0] == 2 and block % 2 == 0 and block < LANE:
+    fits = fits and args[8].shape[0] == 2 and block % 2 == 0 and block < LANE
+    if fits and args[5].shape[0] <= 256:
         return on_device_scatter(*args)
     return on_device_gather(*args)
 

time: 602 us -> 524 us (0.87)
  blocking collectives: 59.2 us -> 0 us
  waiting for transfers between devices: 202 us -> 145 us
  other arithmetic: 32.3 us -> 53.5 us
  Pallas kernels: 152 us -> 159 us
    all_gather x1 -> x0, blocking collectives: 59.2 us -> none  [on_device_scatter(): lax.all_gather(jnp.stack([pair_i, pair_j]), 'pair', axis=1, tiled=True)]
    ppermute x12, waiting for transfers between devices: 152 us -> 96.2 us  [across(): return lax.ppermute(x, 'pair', [(t, t ^ bit) for t in range(count)])]
    unnamed x48 -> x76, local copies, waits for them, and re-layouts: 24.8 us -> 5.33 us
    select_n x17 -> x18, other arithmetic: 20.6 us -> 37.4 us  [the longest x3 12.5 us: block(): return jnp.where(self.from_here(0)[w], pick(kept, beta), pick(came, beta))]
    optimization_barrier x0 -> x1, local copies, waits for them, and re-layouts: none -> 14 us  [after(): return lax.optimization_barrier((x,) + others)[0]]
    slice x4 -> x12, local copies, waits for them, and re-layouts: 6.38 us -> 17.8 us  [the longest x5 15.6 us: on_device_scatter(): amps[1:, :, :, :, start:start + size]]
    pallas_call x3 -> x6, Pallas kernels: 152 us -> 159 us  [triples_call(): pl.pallas_call(functools.partial(triples_kernel, last), grid=(groups,), i...]
  transfers between devices with their start and end apart: 24 -> 24, of which waited for: 13 -> 9; matrix products, arithmetic and copies ran while one was open for 21% -> 29% of each run, Pallas kernels for 7% -> 17%
where the time goes in v2:
time: 524 us; the launch traced here: 515 us
  Pallas kernels  159 us (30%)
  waiting for transfers between devices  145 us (28%)
  local copies, waits for them, and re-layouts  100 us (19%)
  other arithmetic  53.5 us (10%)
  starting transfers between devices  33.6 us (6%)
  matrix products  20.6 us (4%)
    pallas_call x6, Pallas kernels, triples_call(): pl.pallas_call(functools.partial(triples_kernel, last), grid=(groups,), i...  159 us
    ppermute x12, waiting for transfers between devices, across(): return lax.ppermute(x, 'pair', [(t, t ^ bit) for t in range(count)])  96.2 us
    all_to_all x1, waiting for transfers between devices, on_device_scatter(): lax.all_to_all(total.reshape(chips, local_pairs, share), 'pair', 0, 0, ti...  47 us
    dot_general x3, matrix products, on_device_scatter(): jnp.einsum('wgqab,ae->wgbqe', amps[1:, :, :, :, start:start + size], spread)  17.7 us
    ppermute x12, starting transfers between devices, across(): return lax.ppermute(x, 'pair', [(t, t ^ bit) for t in range(count)])  16.2 us
    slice x5, local copies, waits for them, and re-layouts, on_device_scatter(): amps[1:, :, :, :, start:start + size]  15.6 us
    optimization_barrier x1, local copies, waits for them, and re-layouts, after(): return lax.optimization_barrier((x,) + others)[0]  14 us
    select_n x3, other arithmetic, block(): return jnp.where(self.from_here(0)[w], pick(kept, beta), pick(came, beta))  12.5 us
  transfers between devices with their start and end apart: 24, of which 9 were waited for; matrix products, arithmetic and copies ran while one was open for 29% of the time, Pallas kernels for 17%

profile of v2, /device:TPU:12, one launch (start us, length us, event | category | flops | bytes accessed | tf_op | source)
XLA Modules:
  0.0 515.0 jit_solution(6585453716628323468)
XLA Ops:
  0.0 3.7 slice.210
  3.7 2.6 dynamic-slice_bitcast_fusion.2
  6.4 3.6 fusion.87
  10.0 1.6 dynamic-slice_bitcast_fusion.1
  13.8 1.5 dynamic-slice_bitcast_fusion
  21.4 8.0 %gather_fusion.4 = bf16[240,3872]{1,0:T(8,128)(2,1)S(1)} fusion(bf16[5,8,3872]{2,1,0:T(8,128)(2,1)S(1)} %constant_dynamic-slice_fusion, s32[240]{0:T(256)S(1)} %reshape.604), kind=kCustom, calls=%fused_computation.4 | custom fusion | bytes 3719040 | tf_op jit(solution)/shard_map/gather | solution.py:311
  29.4 1.7 reshape.562
  32.6 3.4 pad_maximum_fusion
  36.0 4.4 bitcast_select_fusion
  40.4 7.6 %all-to-all-start = ((bf16[16,16,3872]{2,1,0:T(8,128)(2,1)}), bf16[16,16,3872]{2,1,0:T(8,128)(2,1)S(1)}, u32[]{:S(2)}, u32[]{:S(2)}) async-start(bf16[16,16,3872]{2,1,0:T(8,128)(2,1)} %pad_maximum_fusion), calls=%async_computation | async-start | bytes 4063232 | tf_op jit(solution)/shard_map/all_to_all | solution.py:317
  48.0 1.5 collective-permute-start.3
  52.7 1.5 fusion.36
  54.2 3.9 bitcast_select_fusion.5
  58.2 3.9 bitcast_select_fusion.2
  62.0 52.7 %collective-permute-done.3 = bf16[4,88,2816]{2,1,0:T(8,128)(2,1)} collective-permute-done((bf16[4,88,2816]{2,1,0:T(8,128)(2,1)}, bf16[4,88,2816]{2,1,0:T(8,128)(2,1)}, u32[]{:S(2)}, u32[]{:S(2)}) %collective-permute-start.3) | collective-permute-done | bytes 1982496 | tf_op jit(solution)/shard_map/ppermute | solution.py:219
  115.2 3.9 dynamic-slice_select_fusion.11
  119.3 1.5 pad_maximum_fusion.1
  121.6 1.5 maximum_bitcast_fusion
  123.1 14.0 %copy.132 = bf16[16,16,3872]{0,1,2:T(8,128)(2,1)} copy(bf16[16,16,3872]{2,1,0:T(8,128)(2,1)S(1)} %all-to-all-done) | data formatting | bytes 3964928 | tf_op jit(solution)/shard_map/optimization_barrier | solution.py:227
  140.0 1.2 gather_fusion.10
  141.4 1.2 gather_fusion.6
  143.9 3.0 gather_fusion.5
  146.9 7.3 %reshape.565 = bf16[3,5,16,44,88]{4,3,2,1,0:T(8,128)(2,1)} reshape(bf16[240,3872]{1,0:T(8,128)(2,1)} %gather_fusion.5) | data formatting | bytes 3717120 | tf_op jit(solution)/shard_map/reshape | solution.py:334
  157.9 2.8 fusion.88
  160.7 5.1 dynamic-slice_select_fusion.3
  166.0 1.5 pad_maximum_fusion.2
  168.7 2.7 fusion.20
  171.4 1.3 collective-permute-start.8
  172.7 4.4 copy.155
  181.3 6.8 %convolution_bitcast_fusion.1.refs_4_ = bf16[2,5,32,16,768]{4,3,2,1,0:T(8,128)(2,1)} fusion(bf16[2,5,16,44,32]{3,2,4,1,0:T(8,128)(2,1)} %copy.155, s32[768]{0:T(1024)S(1)} %get-tuple-element.106, pred[768]{0:T(1024)(128)(4,1)S(1)} %iota_compare_fusion.6), kind=kOutput, calls=%fused_computation.15 | convolution fusion | flops 346097664 | bytes 8318720 | tf_op jit(solution)/shard_map/wgqab,ae->wgbqe/dot_general | solution.py:368
  188.1 2.1 collective-permute-start.5
  190.4 3.6 collective-permute-done.8
  194.0 17.7 %collective-permute-done.12 = bf16[2,2,88,2816]{3,2,1,0:T(8,128)(2,1)} collective-permute-done((bf16[2,2,88,2816]{3,2,1,0:T(8,128)(2,1)}, bf16[2,2,88,2816]{3,2,1,0:T(8,128)(2,1)}, u32[]{:S(2)}, u32[]{:S(2)}) %collective-permute-start.12) | collective-permute-done | bytes 1982496 | tf_op jit(solution)/shard_map/ppermute | solution.py:219
  211.7 3.9 fusion.17
  217.1 1.9 slice.222
  219.0 1.7 squeeze.226
  220.7 1.3 reshape.564
  222.0 2.2 copy.134
  224.2 4.3 copy.160
  228.5 2.2 copy.162
  232.0 6.7 %convolution_bitcast_fusion.refs_4_ = bf16[2,5,32,16,768]{4,3,2,1,0:T(8,128)(2,1)} fusion(bf16[2,5,16,44,32]{3,2,4,1,0:T(8,128)(2,1)} %copy.160, s32[768]{0:T(1024)S(1)} %get-tuple-element.106, pred[768]{0:T(1024)(128)(4,1)S(1)} %iota_compare_fusion.6), kind=kOutput, calls=%fused_computation.14 | convolution fusion | flops 346097664 | bytes 8318720 | tf_op jit(solution)/shard_map/wgqab,ae->wgbqe/dot_general | solution.py:368
  239.8 1.4 collective-permute-start.10
  241.2 3.5 dynamic-slice_select_fusion.19
  244.9 18.5 %collective-permute-done.10 = bf16[88,2816]{1,0:T(8,128)(2,1)S(1)} collective-permute-done((bf16[88,2816]{1,0:T(8,128)(2,1)S(1)}, bf16[88,2816]{1,0:T(8,128)(2,1)S(1)}, u32[]{:S(2)}, u32[]{:S(2)}) %collective-permute-start.10) | collective-permute-done | bytes 495648 | tf_op jit(solution)/shard_map/ppermute | solution.py:219
  264.3 1.5 collective-permute-start.11
  266.0 1.2 collective-permute-start.6
  267.4 1.3 collective-permute-start.15
  269.6 28.1 %triples.6.refs_9_ = f32[5,88,768]{2,1,0:T(8,128)S(1)} custom-call(f32[1,32]{1,0:T(1,128)S(1)} %get-tuple-element.87.refs_0_, bf16[2,32,88,128]{3,2,1,0:T(8,128)(2,1)S(1)} %bitcast.212, bf16[2,88,2816]{2,1,0:T(8,128)(2,1)S(1)} %pad_maximum_fusion.4.refs_2_, bf16[5,128,768]{2,1,0:T(8,128)(2,1)S(1)} %pad.13.refs_3_, ...), custom_call_target="tpu_custom_call" | custom-call | flops 29758586880 | bytes 10297344 | tf_op jit(solution)/shard_map/triples/pallas_call | solution.py:194
  297.7 3.7 collective-permute-done.6
  301.5 1.7 fusion.14
  305.2 3.7 collective-permute-start.19
  309.0 28.5 %triples.7.refs_9_ = f32[5,88,768]{2,1,0:T(8,128)S(1)} custom-call(f32[1,32]{1,0:T(1,128)S(1)} %get-tuple-element.86.refs_0_, bf16[2,32,88,128]{3,2,1,0:T(8,128)(2,1)S(1)} %bitcast.213, bf16[2,88,2816]{2,1,0:T(8,128)(2,1)S(1)} %pad_maximum_fusion.4.refs_2_, bf16[5,128,768]{2,1,0:T(8,128)(2,1)S(1)} %pad.13.refs_3_, ...), custom_call_target="tpu_custom_call" | custom-call | flops 29758586880 | bytes 10297344 | tf_op jit(solution)/shard_map/triples/pallas_call | solution.py:194
  341.7 28.5 %triples.8.refs_9_ = f32[5,88,768]{2,1,0:T(8,128)S(1)} custom-call(f32[1,32]{1,0:T(1,128)S(1)} %get-tuple-element.85.refs_0_, bf16[2,32,88,128]{3,2,1,0:T(8,128)(2,1)S(1)} %bitcast.210, bf16[2,88,2816]{2,1,0:T(8,128)(2,1)S(1)} %pad_maximum_fusion.5.refs_2_, bf16[5,128,768]{2,1,0:T(8,128)(2,1)S(1)} %pad.13.refs_3_, ...), custom_call_target="tpu_custom_call" | custom-call | flops 29758586880 | bytes 10297344 | tf_op jit(solution)/shard_map/triples/pallas_call | solution.py:194
  371.4 4.2 convolution_bitcast_fusion.2.refs_4_
  376.3 28.5 %triples.9.refs_9_ = f32[5,88,768]{2,1,0:T(8,128)S(1)} custom-call(f32[1,32]{1,0:T(1,128)S(1)} %get-tuple-element.84.refs_0_, bf16[2,32,88,128]{3,2,1,0:T(8,128)(2,1)S(1)} %bitcast.211, bf16[2,88,2816]{2,1,0:T(8,128)(2,1)S(1)} %pad_maximum_fusion.5.refs_2_, bf16[5,128,768]{2,1,0:T(8,128)(2,1)S(1)} %pad.13.refs_3_, ...), custom_call_target="tpu_custom_call" | custom-call | flops 29758586880 | bytes 10297344 | tf_op jit(solution)/shard_map/triples/pallas_call | solution.py:194
  404.8 2.7 copy-done.2
  407.5 21.9 %triples.10.refs_9_ = f32[5,88,768]{2,1,0:T(8,128)S(1)} custom-call(f32[1,24]{1,0:T(1,128)S(1)} %get-tuple-element.88.refs_0_, bf16[2,24,88,128]{3,2,1,0:T(8,128)(2,1)S(1)} %bitcast.214, bf16[2,88,2112]{2,1,0:T(8,128)(2,1)S(1)} %pad_maximum_fusion.6.refs_2_, bf16[5,128,768]{2,1,0:T(8,128)(2,1)S(1)} %pad.13.refs_3_, ...), custom_call_target="tpu_custom_call" | custom-call | flops 22318940160 | bytes 7723008 | tf_op jit(solution)/shard_map/triples/pallas_call | solution.py:194
  429.4 23.2 %triples.11 = f32[5,768,88]{2,1,0:T(8,128)S(1)} custom-call(f32[1,24]{1,0:T(1,128)S(1)} %get-tuple-element.89.refs_0_, bf16[2,24,88,128]{3,2,1,0:T(8,128)(2,1)S(1)} %bitcast.215, bf16[2,88,2112]{2,1,0:T(8,128)(2,1)S(1)} %pad_maximum_fusion.6.refs_2_, bf16[5,128,768]{2,1,0:T(8,128)(2,1)S(1)} %pad.13.refs_3_, bf16[2,5,24,16,768]{4,3,2,1,0:T(8,128)(2,1)S(1)} %copy-done.2, ...), custom_call_target="tpu_custom_call" | custom-call | flops 22318940160 | bytes 7723008 | tf_op jit(solution)/shard_map/triples/pallas_call | solution.py:194
  452.6 1.3 slice.223
  453.9 1.9 reshape.568
  457.0 1.5 reshape.569
  458.5 6.2 %all-to-all-start.1 = ((f32[16,5,3872]{2,1,0:T(8,128)}), f32[16,5,3872]{2,1,0:T(8,128)S(1)}, u32[]{:S(2)}, u32[]{:S(2)}) async-start(f32[16,5,3872]{2,1,0:T(8,128)} %reshape.569), calls=%async_computation.1 | async-start | bytes 4063232 | tf_op jit(solution)/shard_map/all_to_all | solution.py:410
  464.8 47.0 %all-to-all-done.1 = f32[16,5,3872]{2,1,0:T(8,128)S(1)} async-done(((f32[16,5,3872]{2,1,0:T(8,128)}), f32[16,5,3872]{2,1,0:T(8,128)S(1)}, u32[]{:S(2)}, u32[]{:S(2)}) %all-to-all-start.1) | async-done | bytes 1239072 | tf_op jit(solution)/shard_map/all_to_all | solution.py:410
  512.2 2.4 gather_fusion.13
  (234 shorter events, 41.8 us)
Async XLA Ops:
  0.0 20.6 %copy-start = (bf16[5,8,7744]{2,1,0:T(8,128)(2,1)S(1)}, bf16[5,8,7744]{2,1,0:T(8,128)(2,1)}, u32[]{:S(2)}) copy-start(bf16[5,8,7744]{2,1,0:T(8,128)(2,1)} %param.10) | copy-start | bytes 1858564
  6.4 47.9 %collective-permute-start = (bf16[4,88,2112]{2,1,0:T(8,128)(2,1)}, bf16[4,88,2112]{2,1,0:T(8,128)(2,1)}, u32[]{:S(2)}, u32[]{:S(2)}) collective-permute-start(bf16[4,88,2112]{2,1,0:T(8,128)(2,1)} %dynamic-slice_bitcast_fusion.2), channel_id=1, source_target_pairs={{0,1},{1,0},{2,3},{3,2},{4,5},{5,4},{6,7},{7,6},{8,9},{9,8},{10,11... | collective-permute-start | bytes 4460552 | tf_op jit(solution)/shard_map/ppermute | solution.py:214
  10.0 2.6 copy-start.9
  10.0 3.8 copy-start.11
  12.6 45.5 %collective-permute-start.1 = (bf16[4,88,2816]{2,1,0:T(8,128)(2,1)}, bf16[4,88,2816]{2,1,0:T(8,128)(2,1)}, u32[]{:S(2)}, u32[]{:S(2)}) collective-permute-start(bf16[4,88,2816]{2,1,0:T(8,128)(2,1)} %dynamic-slice_bitcast_fusion.1), channel_id=1, source_target_pairs={{0,1},{1,0},{2,3},{3,2},{4,5},{5,4},{6,7},{7,6},{8,9},{9,8},{10,11... | collective-permute-start | bytes 5947400 | tf_op jit(solution)/shard_map/ppermute | solution.py:214
  13.8 2.0 copy-start.28
  13.8 2.1 copy-start.35
  13.8 2.1 copy-start.3
  13.8 2.8 copy-start.29
  13.8 4.0 copy-start.33
  13.8 4.0 copy-start.34
  15.2 5.6 %copy-start.32 = (s32[2]{0:T(128)S(1)}, s32[2]{0:T(128)}, u32[]{:S(2)}) copy-start(s32[2]{0:T(128)} %param.19) | copy-start | bytes 28
  15.2 20.8 %collective-permute-start.2 = (bf16[4,88,2816]{2,1,0:T(8,128)(2,1)}, bf16[4,88,2816]{2,1,0:T(8,128)(2,1)}, u32[]{:S(2)}, u32[]{:S(2)}) collective-permute-start(bf16[4,88,2816]{2,1,0:T(8,128)(2,1)} %dynamic-slice_bitcast_fusion), channel_id=1, source_target_pairs={{0,1},{1,0},{2,3},{3,2},{4,5},{5,4},{6,7},{7,6},{8,9},{9,8},{10,11... | collective-permute-start | bytes 5947400 | tf_op jit(solution)/shard_map/ppermute | solution.py:214
  15.8 37.0 %collective-permute-start.13 = (bf16[2,30,30,88]{3,0,2,1:T(2,128)(2,1)S(1)}, bf16[2,30,30,88]{3,0,2,1:T(2,128)(2,1)}, u32[]{:S(2)}, u32[]{:S(2)}) collective-permute-start(bf16[2,30,30,88]{3,0,2,1:T(2,128)(2,1)S(1)} %copy-done.28), channel_id=1, source_target_pairs={{0,1},{1,0},{2,3},{3,2},{4,5},{5,4},{6,7},{7,6},{8,9},{9,8},{10,11... | collective-permute-start | bytes 950408 | tf_op jit(solution)/shard_map/ppermute | solution.py:214
  20.8 0.5 copy-start.30
  40.4 11.7 %copy-start.4 = (f32[30]{0:T(128)S(1)}, f32[30]{0:T(128)}, u32[]{:S(2)}) copy-start(f32[30]{0:T(128)} %param.13) | copy-start | bytes 364
  40.4 82.6 %all-to-all-start = ((bf16[16,16,3872]{2,1,0:T(8,128)(2,1)}), bf16[16,16,3872]{2,1,0:T(8,128)(2,1)S(1)}, u32[]{:S(2)}, u32[]{:S(2)}) async-start(bf16[16,16,3872]{2,1,0:T(8,128)(2,1)} %pad_maximum_fusion), calls=%async_computation | async-start | bytes 4063232 | tf_op jit(solution)/shard_map/all_to_all | solution.py:317
  48.0 66.8 %collective-permute-start.3 = (bf16[4,88,2816]{2,1,0:T(8,128)(2,1)}, bf16[4,88,2816]{2,1,0:T(8,128)(2,1)}, u32[]{:S(2)}, u32[]{:S(2)}) collective-permute-start(bf16[4,88,2816]{2,1,0:T(8,128)(2,1)} %get-tuple-element.39), channel_id=1, source_target_pairs={{0,2},{2,0},{4,6},{6,4},{8,10},{10,8},{12,14},{14,12},{16,18},{18,... | collective-permute-start | bytes 5947400 | tf_op jit(solution)/shard_map/ppermute | solution.py:219
  54.2 3.9 copy-start.10
  58.1 57.1 %copy-start.7 = (bf16[4,88,2816]{2,1,0:T(8,128)(2,1)S(1)}, bf16[4,88,2816]{2,1,0:T(8,128)(2,1)}, u32[]{:S(2)}) copy-start(bf16[4,88,2816]{2,1,0:T(8,128)(2,1)} %get-tuple-element.38) | copy-start | bytes 5947396
  114.8 45.9 %collective-permute-start.4 = (bf16[4,88,2816]{2,1,0:T(8,128)(2,1)}, bf16[4,88,2816]{2,1,0:T(8,128)(2,1)}, u32[]{:S(2)}, u32[]{:S(2)}) collective-permute-start(bf16[4,88,2816]{2,1,0:T(8,128)(2,1)} %get-tuple-element.18), channel_id=1, source_target_pairs={{0,2},{2,0},{4,6},{6,4},{8,10},{10,8},{12,14},{14,12},{16,18},{18,... | collective-permute-start | bytes 5947400 | tf_op jit(solution)/shard_map/ppermute | solution.py:219
  120.8 47.9 %collective-permute-start.7 = (bf16[2,2,88,2816]{3,2,1,0:T(8,128)(2,1)}, bf16[2,2,88,2816]{3,2,1,0:T(8,128)(2,1)}, u32[]{:S(2)}, u32[]{:S(2)}) collective-permute-start(bf16[2,2,88,2816]{3,2,1,0:T(8,128)(2,1)} %pad_maximum_fusion.1), channel_id=1, source_target_pairs={{0,4},{2,6},{4,0},{6,2},{8,12},{10,14},{12,8},{14,10},{16,20},{18,... | collective-permute-start | bytes 5947400 | tf_op jit(solution)/shard_map/ppermute | solution.py:219
  155.9 2.0 copy-start.5
  157.9 2.8 copy-start.8
  166.0 2.7 copy-start.13
  166.0 2.7 copy-start.14
  167.5 44.1 %collective-permute-start.12 = (bf16[2,2,88,2816]{3,2,1,0:T(8,128)(2,1)}, bf16[2,2,88,2816]{3,2,1,0:T(8,128)(2,1)}, u32[]{:S(2)}, u32[]{:S(2)}) collective-permute-start(bf16[2,2,88,2816]{3,2,1,0:T(8,128)(2,1)} %pad_maximum_fusion.2), channel_id=1, source_target_pairs={{0,4},{2,6},{4,0},{6,2},{8,12},{10,14},{12,8},{14,10},{16,20},{18,... | collective-permute-start | bytes 5947400 | tf_op jit(solution)/shard_map/ppermute | solution.py:219
  171.4 22.6 %collective-permute-start.8 = (bf16[2,88,2816]{2,1,0:T(8,128)(2,1)}, bf16[2,88,2816]{2,1,0:T(8,128)(2,1)}, u32[]{:S(2)}, u32[]{:S(2)}) collective-permute-start(bf16[2,88,2816]{2,1,0:T(8,128)(2,1)} %fusion.20), channel_id=1, source_target_pairs={{0,8},{2,10},{4,12},{6,14},{8,0},{10,2},{12,4},{14,6},{16,24},{18,... | collective-permute-start | bytes 2973704 | tf_op jit(solution)/shard_map/ppermute | solution.py:219
  181.3 8.9 %copy-start.22 = (bf16[1,88,2816]{2,1,0:T(8,128)(2,1)S(1)}, bf16[1,88,2816]{2,1,0:T(8,128)(2,1)}, u32[]{:S(2)}) copy-start(bf16[1,88,2816]{2,1,0:T(8,128)(2,1)} %get-tuple-element.46) | copy-start | bytes 1486852
  181.3 8.9 %copy-start.23 = (bf16[1,88,2816]{2,1,0:T(8,128)(2,1)S(1)}, bf16[1,88,2816]{2,1,0:T(8,128)(2,1)}, u32[]{:S(2)}) copy-start(bf16[1,88,2816]{2,1,0:T(8,128)(2,1)} %get-tuple-element.47) | copy-start | bytes 1486852
  181.3 8.9 %copy-start.24 = (bf16[1,88,2816]{2,1,0:T(8,128)(2,1)S(1)}, bf16[1,88,2816]{2,1,0:T(8,128)(2,1)}, u32[]{:S(2)}) copy-start(bf16[1,88,2816]{2,1,0:T(8,128)(2,1)} %get-tuple-element.48) | copy-start | bytes 1486852
  181.3 8.9 %copy-start.25 = (bf16[1,88,2816]{2,1,0:T(8,128)(2,1)S(1)}, bf16[1,88,2816]{2,1,0:T(8,128)(2,1)}, u32[]{:S(2)}) copy-start(bf16[1,88,2816]{2,1,0:T(8,128)(2,1)} %get-tuple-element.49) | copy-start | bytes 1486852
  188.1 53.1 %collective-permute-start.5 = (bf16[4,88,2112]{2,1,0:T(8,128)(2,1)}, bf16[4,88,2112]{2,1,0:T(8,128)(2,1)}, u32[]{:S(2)}, u32[]{:S(2)}) collective-permute-start(bf16[4,88,2112]{2,1,0:T(8,128)(2,1)} %get-tuple-element.19), channel_id=1, source_target_pairs={{0,2},{2,0},{4,6},{6,4},{8,10},{10,8},{12,14},{14,12},{16,18},{18,... | collective-permute-start | bytes 4460552 | tf_op jit(solution)/shard_map/ppermute | solution.py:219
  190.4 25.2 %copy-start.15 = (bf16[1,2,88,2816]{3,2,1,0:T(8,128)(2,1)}, bf16[1,2,88,2816]{3,2,1,0:T(8,128)(2,1)S(1)}, u32[]{:S(2)}) copy-start(bf16[1,2,88,2816]{3,2,1,0:T(8,128)(2,1)S(1)} %get-tuple-element.113) | copy-start | bytes 2973700
  190.4 25.2 %copy-start.17 = (bf16[1,2,88,2816]{3,2,1,0:T(8,128)(2,1)}, bf16[1,2,88,2816]{3,2,1,0:T(8,128)(2,1)S(1)}, u32[]{:S(2)}) copy-start(bf16[1,2,88,2816]{3,2,1,0:T(8,128)(2,1)S(1)} %get-tuple-element.114) | copy-start | bytes 2973700
  211.7 5.4 %copy-start.6 = (bf16[3,5,16,44,88]{4,3,2,1,0:T(8,128)(2,1)S(1)}, bf16[3,5,16,44,88]{4,3,2,1,0:T(8,128)(2,1)}, u32[]{:S(2)}) copy-start(bf16[3,5,16,44,88]{4,3,2,1,0:T(8,128)(2,1)} %reshape.565) | copy-start | bytes 5575684
  215.6 1.5 copy-start.20
  216.5 22.2 %collective-permute-start.9 = (bf16[88,2816]{1,0:T(8,128)(2,1)}, bf16[88,2816]{1,0:T(8,128)(2,1)}, u32[]{:S(2)}, u32[]{:S(2)}) collective-permute-start(bf16[88,2816]{1,0:T(8,128)(2,1)} %dynamic-slice_bitcast_fusion.4), channel_id=1, source_target_pairs={{0,1},{1,0},{2,3},{3,2},{4,5},{5,4},{6,7},{7,6},{8,9},{9,8},{10,11... | collective-permute-start | bytes 1486856 | tf_op jit(solution)/shard_map/ppermute | solution.py:214
  217.1 1.9 slice-start.2
  224.2 4.3 copy-start.19
  231.9 6.8 %copy-start.21 = (bf16[2,88,2816]{2,1,0:T(8,128)(2,1)S(1)}, bf16[2,88,2816]{2,1,0:T(8,128)(2,1)}, u32[]{:S(2)}) copy-start(bf16[2,88,2816]{2,1,0:T(8,128)(2,1)} %copy-done.20) | copy-start | bytes 2973700
  232.0 9.3 %copy-start.12 = (bf16[4,88,2112]{2,1,0:T(8,128)(2,1)S(1)}, bf16[4,88,2112]{2,1,0:T(8,128)(2,1)}, u32[]{:S(2)}) copy-start(bf16[4,88,2112]{2,1,0:T(8,128)(2,1)} %get-tuple-element.40) | copy-start | bytes 4460548
  239.8 23.6 %collective-permute-start.10 = (bf16[88,2816]{1,0:T(8,128)(2,1)S(1)}, bf16[88,2816]{1,0:T(8,128)(2,1)S(1)}, u32[]{:S(2)}, u32[]{:S(2)}) collective-permute-start(bf16[88,2816]{1,0:T(8,128)(2,1)S(1)} %bitcast_select_fusion.8), channel_id=1, source_target_pairs={{0,16},{2,18},{4,20},{6,22},{8,24},{10,26},{12,28},{14,30},{16,0},... | collective-permute-start | bytes 1486856 | tf_op jit(solution)/shard_map/ppermute | solution.py:219
  263.4 6.2 %slice-start = ((s8[7864320]{0:T(1024)(128)(4,1)}), s8[4194304]{0:T(1024)(128)(4,1)S(1)}, s32[]{:S(2)}) async-start(s8[7864320]{0:T(1024)(128)(4,1)} %bitcast.216), calls=%async_computation.2 | async-start | bytes 8388608
  264.3 4.4 collective-permute-start.11
  266.0 1.4 copy-start.26
  266.0 35.5 %collective-permute-start.6 = (bf16[2,2,88,2112]{3,2,1,0:T(8,128)(2,1)S(1)}, bf16[2,2,88,2112]{3,2,1,0:T(8,128)(2,1)S(1)}, u32[]{:S(2)}, u32[]{:S(2)}) collective-permute-start(bf16[2,2,88,2112]{3,2,1,0:T(8,128)(2,1)S(1)} %pad_maximum_fusion.3), channel_id=1, source_target_pairs={{0,4},{2,6},{4,0},{6,2},{8,12},{10,14},{12,8},{14,10},{16,20},{18,... | collective-permute-start | bytes 4460552 | tf_op jit(solution)/shard_map/ppermute | solution.py:219
  267.2 2.4 slice-start.1
  267.4 34.1 %collective-permute-start.15 = (bf16[2,88,2816]{2,1,0:T(8,128)(2,1)S(1)}, bf16[2,88,2816]{2,1,0:T(8,128)(2,1)S(1)}, u32[]{:S(2)}, u32[]{:S(2)}) collective-permute-start(bf16[2,88,2816]{2,1,0:T(8,128)(2,1)S(1)} %copy-done.26), channel_id=1, source_target_pairs={{0,8},{2,10},{4,12},{6,14},{8,0},{10,2},{12,4},{14,6},{16,24},{18,... | collective-permute-start | bytes 2973704 | tf_op jit(solution)/shard_map/ppermute | solution.py:219
  269.6 31.9 %copy-start.16 = (bf16[1,2,88,2816]{3,2,1,0:T(8,128)(2,1)S(1)}, bf16[1,2,88,2816]{3,2,1,0:T(8,128)(2,1)}, u32[]{:S(2)}) copy-start(bf16[1,2,88,2816]{3,2,1,0:T(8,128)(2,1)} %copy-done.15) | copy-start | bytes 2973700
  269.6 31.9 %copy-start.18 = (bf16[1,2,88,2816]{3,2,1,0:T(8,128)(2,1)S(1)}, bf16[1,2,88,2816]{3,2,1,0:T(8,128)(2,1)}, u32[]{:S(2)}) copy-start(bf16[1,2,88,2816]{3,2,1,0:T(8,128)(2,1)} %copy-done.17) | copy-start | bytes 2973700
  303.2 1.9 collective-permute-start.16
  303.7 33.8 %collective-permute-start.14 = (bf16[2,88,2112]{2,1,0:T(8,128)(2,1)S(1)}, bf16[2,88,2112]{2,1,0:T(8,128)(2,1)S(1)}, u32[]{:S(2)}, u32[]{:S(2)}) collective-permute-start(bf16[2,88,2112]{2,1,0:T(8,128)(2,1)S(1)} %fusion.27), channel_id=1, source_target_pairs={{0,8},{2,10},{4,12},{6,14},{8,0},{10,2},{12,4},{14,6},{16,24},{18,... | collective-permute-start | bytes 2230280 | tf_op jit(solution)/shard_map/ppermute | solution.py:219
  305.2 32.8 %collective-permute-start.19 = (bf16[88,2816]{1,0:T(8,128)(2,1)S(1)}, bf16[88,2816]{1,0:T(8,128)(2,1)S(1)}, u32[]{:S(2)}, u32[]{:S(2)}) collective-permute-start(bf16[88,2816]{1,0:T(8,128)(2,1)S(1)} %bitcast_select_fusion.7), channel_id=1, source_target_pairs={{0,16},{2,18},{4,20},{6,22},{8,24},{10,26},{12,28},{14,30},{16,0},... | collective-permute-start | bytes 1486856 | tf_op jit(solution)/shard_map/ppermute | solution.py:219
  338.0 1.8 collective-permute-start.17
  338.8 2.0 collective-permute-start.20
  339.8 30.4 %collective-permute-start.18 = (bf16[88,2112]{1,0:T(8,128)(2,1)S(1)}, bf16[88,2112]{1,0:T(8,128)(2,1)S(1)}, u32[]{:S(2)}, u32[]{:S(2)}) collective-permute-start(bf16[88,2112]{1,0:T(8,128)(2,1)S(1)} %bitcast_select_fusion.10), channel_id=1, source_target_pairs={{0,16},{2,18},{4,20},{6,22},{8,24},{10,26},{12,28},{14,30},{16,0},... | collective-permute-start | bytes 1115144 | tf_op jit(solution)/shard_map/ppermute | solution.py:219
  341.7 29.7 %copy-start.27 = (bf16[2,5,16,44,24]{3,2,4,1,0:T(8,128)(2,1)S(1)}, bf16[2,5,16,44,24]{3,2,4,1,0:T(8,128)(2,1)}, u32[]{:S(2)}) copy-start(bf16[2,5,16,44,24]{3,2,4,1,0:T(8,128)(2,1)} %copy.162) | copy-start | bytes 1013764
  370.9 4.7 collective-permute-start.21
  404.8 2.7 copy-start.2
  458.5 6.2 %copy-start.31 = (s32[5]{0:T(128)S(1)}, s32[5]{0:T(128)}, u32[]{:S(2)}) copy-start(s32[5]{0:T(128)} %copy-done.30) | copy-start | bytes 64
  458.5 53.3 %all-to-all-start.1 = ((f32[16,5,3872]{2,1,0:T(8,128)}), f32[16,5,3872]{2,1,0:T(8,128)S(1)}, u32[]{:S(2)}, u32[]{:S(2)}) async-start(f32[16,5,3872]{2,1,0:T(8,128)} %reshape.569), calls=%async_computation.1 | async-start | bytes 4063232 | tf_op jit(solution)/shard_map/all_to_all | solution.py:410
  511.9 2.6 copy-start.1
